TPU v7x, 1024 devices: a whole 8x8x8 slice. The times are simulated.
1024 devices in a mesh: dp: 8 (over z_lo, core), hidden: 16 (over x, z_hi), mp: 8 (over y).
Axes of the slice: x: 8, y: 8, z: 8 (z_hi: 2, z_lo: 4; z = z_hi * 4 + z_lo), core: 2. Of those that a mesh axis runs over, the one named last changes fastest.
Arguments:
- activations: bfloat16 [4096, 26624], P('dp', 'hidden'), may hold values from -6 to 6
- weight: bfloat16 [26624, 8192], P('hidden', 'mp'), may hold values from -0.0390625 to 0.0390625
- out_grad: bfloat16 [4096, 8192], P(('dp', 'hidden'), 'mp'), may hold values from -0.25 to 0.25
- momentum: float32 [8, 3328, 8192], P('dp', 'hidden', 'mp'), may hold values from -6 to 6
Outputs:
- output: bfloat16 [4096, 8192], P(('dp', 'hidden'), 'mp')
- new_momentum: float32 [8, 3328, 8192], P('dp', 'hidden', 'mp')
- new_weight: bfloat16 [8, 3328, 8192], P('dp', 'hidden', 'mp')
All inputs are finite; a program needn't handle non-finite values.
Results may differ from a plain program's by a relative error of at most 0.015.
Values may be sent and summed in bfloat16 or wider, within the bound.
No kernel may reach another device: no remote copies, remote signals or barrier semaphores. Data moves between devices by JAX's collectives and lax.ppermute only.
A program may use at most 32 MiB of HBM per device.

v0:
```python
import jax
import jax.numpy as jnp
import numpy as np
from jax import lax
from jax.sharding import Mesh, PartitionSpec as P


momentum_decay = 0.9
step_size = 0.05

SWAP = [(0, 1), (1, 0)]


def after(value, *others):
    return lax.optimization_barrier((value, *others))[0]


def in_order(index, mine, other, axis):
    first, second = jnp.where(index == 0, mine, other), jnp.where(index == 0, other, mine)
    return jnp.stack([first, second], axis=axis)


def step(activations, weight, out_grad, momentum):
    slab_rows = momentum.shape[1]
    tokens, hid = activations.shape
    own_tokens, cols = out_grad.shape
    n_x = tokens // own_tokens // 2
    half = cols // 2
    part = half // 2
    core, z_hi, z_lo = (lax.axis_index(a) for a in ("core", "z_hi", "z_lo"))
    n_z = hid // slab_rows // 2

    sent = out_grad.reshape(own_tokens, 2, 2, part)[:, :, 0].transpose(1, 0, 2)
    sent = jnp.broadcast_to(sent[None, :, None], (n_x, 2, 2, own_tokens, part))
    gathered0 = lax.all_to_all(
        sent.reshape(4 * n_x, own_tokens, part),
        ("x", "core", "z_hi"),
        split_axis=0,
        concat_axis=0,
        tiled=True,
    )

    def second_part(of_core):
        return lax.dynamic_slice_in_dim(out_grad, of_core * half + part, part, 1)

    partner = lax.ppermute(second_part(1 - core), "core", SWAP)
    pair = in_order(core, second_part(core), partner, 0)
    far_pair = lax.ppermute(pair, "z_hi", SWAP)
    quad = in_order(z_hi, pair, far_pair, 1)
    sent = jnp.broadcast_to(quad[None], (n_x, 2, 2, own_tokens, part))
    gathered1 = lax.all_to_all(after(sent, gathered0), "x", split_axis=0, concat_axis=0, tiled=True)

    partner_act = lax.ppermute(after(activations, partner), "core", SWAP)
    both_act = in_order(
        core,
        activations.reshape(n_x, 2 * own_tokens, hid),
        partner_act.reshape(n_x, 2 * own_tokens, hid),
        1,
    ).reshape(2 * tokens, hid)
    both_act = lax.optimization_barrier(both_act)

    partial_out = jnp.dot(activations, weight, preferred_element_type=jnp.float32)
    partial_out = partial_out.astype(jnp.bfloat16).reshape(n_x, 2, own_tokens, cols)
    keep = lax.dynamic_index_in_dim(partial_out, z_hi, 1, keepdims=False)
    give = lax.dynamic_index_in_dim(partial_out, 1 - z_hi, 1, keepdims=False)
    got = lax.ppermute(after(give, far_pair), "z_hi", SWAP)

    own_piece, arrived = [], []
    for p, gathered in enumerate((gathered0, gathered1)):
        local_grad = lax.dot_general(
            both_act,
            gathered.reshape(2 * tokens, part),
            (((0,), (0,)), ((), ())),
            preferred_element_type=jnp.float32,
        )
        slabs = local_grad.astype(jnp.bfloat16).reshape(n_z, 2, slab_rows, part)
        own_piece.append(lax.dynamic_index_in_dim(slabs, z_lo, 0, keepdims=False))
        sent = [
            lax.dynamic_index_in_dim(slabs, (z_lo + d) % n_z, 0, keepdims=False)
            for d in range(1, n_z)
        ]
        if p > 0:
            arrived[-1] = list(lax.optimization_barrier((*arrived[-1], sent[0]))[:-1])
        arrived.append(
            [
                lax.ppermute(s, "z_lo", [(i, (i + d) % n_z) for i in range(n_z)])
                for d, s in enumerate(sent, 1)
            ]
        )
    got = after(got, sent[0])
    paired = (keep.astype(jnp.float32) + got.astype(jnp.float32)).astype(jnp.bfloat16)
    pieces = lax.all_to_all(paired, "x", split_axis=0, concat_axis=0, tiled=True)
    summed = jnp.sum(pieces.astype(jnp.float32), axis=0).astype(jnp.bfloat16)

    own_part, got_part = [], []
    for own, others in zip(own_piece, arrived):
        total = own.astype(jnp.float32)
        for a in others:
            total = total + a.astype(jnp.float32)
        own_part.append(lax.dynamic_index_in_dim(total, core, 0, keepdims=False))
        give = lax.dynamic_index_in_dim(total, 1 - core, 0, keepdims=False).astype(jnp.bfloat16)
        got_part.append(lax.ppermute(give, "core", SWAP).astype(jnp.float32))
    own_half = jnp.concatenate(own_part, axis=1)
    got_half = jnp.concatenate(got_part, axis=1)
    grad_share = jnp.concatenate(
        [jnp.where(core == 0, own_half, got_half), jnp.where(core == 0, got_half, own_half)], axis=1
    )
    new_momentum = momentum_decay * momentum + grad_share[None]
    own_rows = lax.dynamic_slice_in_dim(weight, (z_lo * 2 + core) * slab_rows, slab_rows, 0)
    new_weight = (own_rows.astype(jnp.float32)[None] - step_size * new_momentum).astype(
        jnp.bfloat16
    )
    return (summed, new_momentum, new_weight)


def solution(mesh):
    n_dp, n_hidden, n_mp = (mesh.shape[a] for a in ("dp", "hidden", "mp"))
    grid = np.asarray(mesh.devices).reshape(n_dp // 2, 2, n_hidden // 2, 2, n_mp)
    finer = Mesh(grid, ("z_lo", "core", "x", "z_hi", "mp"))
    dp, hidden = ("z_lo", "core"), ("x", "z_hi")
    return jax.shard_map(
        step,
        mesh=finer,
        in_specs=(P(dp, hidden), P(hidden, "mp"), P(dp + hidden, "mp"), P(dp, hidden, "mp")),
        out_specs=(P(dp + hidden, "mp"), P(dp, hidden, "mp"), P(dp, hidden, "mp")),
        check_vma=False,
    )
```

profile of v0, /device:TPU:1, one launch (start us, length us, event | category | flops | bytes accessed | tf_op | source)
XLA Modules:
  0.0 139.8 jit_solution(15738856506170956786)
XLA Ops:
  0.6 0.7 constant_dynamic-slice_fusion
  1.4 16.0 %collective-permute-start = (bf16[32,256]{1,0:T(8,128)(2,1)S(1)}, bf16[32,256]{1,0:T(8,128)(2,1)S(1)}, u32[]{:S(2)}, u32[]{:S(2)}) collective-permute-start(bf16[32,256]{1,0:T(8,128)(2,1)S(1)} %constant_dynamic-slice_fusion), channel_id=1, source_target_pairs={{0,128},{128,0},{1,129},{129,1},{2,130},{130,2},{3,131},{131,3},{4... | collective-permute-start | bytes 49160 | tf_op jit(solution)/shard_map/ppermute | solution.py:46
  17.4 0.8 collective-permute-done
  18.2 2.2 %collective-permute-start.3 = (bf16[512,1664]{1,0:T(8,128)(2,1)}, bf16[512,1664]{1,0:T(8,128)(2,1)S(1)}, u32[]{:S(2)}, u32[]{:S(2)}) collective-permute-start(bf16[512,1664]{1,0:T(8,128)(2,1)} %param.4), channel_id=1, source_target_pairs={{0,128},{128,0},{1,129},{129,1},{2,130},{130,2},{3,131},{131,3},{4... | collective-permute-start | bytes 5111816 | tf_op jit(solution)/shard_map/ppermute | solution.py:53
  20.4 0.9 reshape.82
  21.3 0.9 broadcast_in_dim.22
  22.2 6.6 %all-to-all-start = ((bf16[32,32,256]{2,1,0:T(8,128)(2,1)}), bf16[32,32,256]{2,1,0:T(8,128)(2,1)}, u32[]{:S(2)}, u32[]{:S(2)}) async-start(bf16[32,32,256]{2,1,0:T(8,128)(2,1)} %bitcast.12), calls=%async_computation | async-start | bytes 1048576 | tf_op jit(solution)/shard_map/all_to_all | solution.py:35
  28.8 5.6 %convolution_convert_fusion.2 = bf16[512,1024]{1,0:T(8,128)(2,1)} fusion(bf16[512,1664]{1,0:T(8,128)(2,1)} %param.4, bf16[1664,1024]{1,0:T(8,128)(2,1)} %param.5), kind=kOutput, calls=%fused_computation.5 | convolution fusion | flops 1745354752 | bytes 6160384 | tf_op jit(solution)/shard_map/dot_general | solution.py:62
  34.4 0.0 copy-start
  34.4 0.9 select_bitcast_fusion.3
  35.2 7.2 %collective-permute-start.1 = (bf16[2,32,256]{2,1,0:T(8,128)(2,1)S(1)}, bf16[2,32,256]{2,1,0:T(8,128)(2,1)S(1)}, u32[]{:S(2)}, u32[]{:S(2)}) collective-permute-start(bf16[2,32,256]{2,1,0:T(8,128)(2,1)S(1)} %pad_maximum_fusion.4), channel_id=1, source_target_pairs={{0,8},{8,0},{1,9},{9,1},{2,10},{10,2},{3,11},{11,3},{4,12},{12,4},... | collective-permute-start | bytes 98312 | tf_op jit(solution)/shard_map/ppermute | solution.py:48
  42.4 1.9 %dynamic-slice_bitcast_fusion = bf16[8,32,1024]{2,1,0:T(8,128)(2,1)} fusion(bf16[8,2,32,1024]{3,2,1,0:T(8,128)(2,1)} %bitcast.72, s32[]{:T(128)S(6)} %select_n.132), kind=kLoop, calls=%fused_computation.14 | loop fusion | bytes 1048580 | tf_op jit(solution)/shard_map/jit(dynamic_index_in_dim)/squeeze | solution.py:65
  44.3 5.3 %collective-permute-done.1 = bf16[2,32,256]{2,1,0:T(8,128)(2,1)S(1)} collective-permute-done((bf16[2,32,256]{2,1,0:T(8,128)(2,1)S(1)}, bf16[2,32,256]{2,1,0:T(8,128)(2,1)S(1)}, u32[]{:S(2)}, u32[]{:S(2)}) %collective-permute-start.1) | collective-permute-done | bytes 32800 | tf_op jit(solution)/shard_map/ppermute | solution.py:48
  49.6 1.9 %collective-permute-start.2 = (bf16[8,32,1024]{2,1,0:T(8,128)(2,1)}, bf16[8,32,1024]{2,1,0:T(8,128)(2,1)}, u32[]{:S(2)}, u32[]{:S(2)}) collective-permute-start(bf16[8,32,1024]{2,1,0:T(8,128)(2,1)} %dynamic-slice_bitcast_fusion), channel_id=1, source_target_pairs={{0,8},{8,0},{1,9},{9,1},{2,10},{10,2},{3,11},{11,3},{4,12},{12,4},... | collective-permute-start | bytes 1572872 | tf_op jit(solution)/shard_map/ppermute | solution.py:66
  51.6 0.0 all-to-all-done
  51.6 0.9 broadcast_in_dim.21
  52.4 6.0 %all-to-all-start.1 = ((bf16[8,2,2,32,256]{4,3,2,1,0:T(8,128)(2,1)}), bf16[8,2,2,32,256]{4,3,2,1,0:T(8,128)(2,1)}, u32[]{:S(2)}, u32[]{:S(2)}) async-start(bf16[8,2,2,32,256]{4,3,2,1,0:T(8,128)(2,1)} %broadcast_in_dim.21), calls=%async_computation.1 | async-start | bytes 1048576 | tf_op jit(solution)/shard_map/all_to_all | solution.py:51
  58.4 0.0 collective-permute-done.3
  58.4 0.0 copy-done
  58.5 0.3 broadcast_select_fusion.1
  58.8 0.3 pad_maximum_fusion
  59.1 2.1 %convolution_convert_fusion = bf16[1664,256]{1,0:T(8,128)(2,1)S(1)} fusion(bf16[1024,1664]{1,0:T(8,128)(2,1)S(1)} %bitcast.70, bf16[1024,256]{1,0:T(8,128)(2,1)} %bitcast.16), kind=kOutput, calls=%fused_computation.1 | convolution fusion | flops 872841216 | bytes 4784128 | tf_op jit(solution)/shard_map/dot_general | solution.py:70
  61.3 0.0 copy-start.3
  61.3 0.9 copy-done.3
  62.2 0.8 dynamic-slice_bitcast_fusion.5
  63.0 4.3 %collective-permute-start.4 = (bf16[2,208,256]{2,1,0:T(8,128)(2,1)}, bf16[2,208,256]{2,1,0:T(8,128)(2,1)}, u32[]{:S(2)}, u32[]{:S(2)}) collective-permute-start(bf16[2,208,256]{2,1,0:T(8,128)(2,1)} %get-tuple-element.23), channel_id=1, source_target_pairs={{0,256},{256,512},{512,768},{768,0},{1,257},{257,513},{513,769},{7... | collective-permute-start | bytes 638984 | tf_op jit(solution)/shard_map/ppermute | solution.py:86
  67.3 5.4 %collective-permute-start.5 = (bf16[2,208,256]{2,1,0:T(8,128)(2,1)}, bf16[2,208,256]{2,1,0:T(8,128)(2,1)}, u32[]{:S(2)}, u32[]{:S(2)}) collective-permute-start(bf16[2,208,256]{2,1,0:T(8,128)(2,1)} %get-tuple-element.22), channel_id=1, source_target_pairs={{0,512},{256,768},{512,0},{768,256},{1,513},{257,769},{513,1},{769... | collective-permute-start | bytes 638984 | tf_op jit(solution)/shard_map/ppermute | solution.py:86
  72.7 2.2 %collective-permute-start.6 = (bf16[2,208,256]{2,1,0:T(8,128)(2,1)}, bf16[2,208,256]{2,1,0:T(8,128)(2,1)}, u32[]{:S(2)}, u32[]{:S(2)}) collective-permute-start(bf16[2,208,256]{2,1,0:T(8,128)(2,1)} %get-tuple-element.21), channel_id=1, source_target_pairs={{0,768},{256,0},{512,256},{768,512},{1,769},{257,1},{513,257},{769... | collective-permute-start | bytes 638984 | tf_op jit(solution)/shard_map/ppermute | solution.py:86
  74.8 0.0 all-to-all-done.1
  74.9 2.1 %convolution_convert_fusion.1 = bf16[1664,256]{1,0:T(8,128)(2,1)S(1)} fusion(bf16[1024,1664]{1,0:T(8,128)(2,1)S(1)} %bitcast.71, bf16[1024,256]{1,0:T(8,128)(2,1)} %bitcast.13), kind=kOutput, calls=%fused_computation.2 | convolution fusion | flops 872841216 | bytes 4784128 | tf_op jit(solution)/shard_map/dot_general | solution.py:70
  77.0 0.0 copy-start.2
  77.0 0.0 copy-start.1
  77.0 0.1 dynamic-slice_bitcast_fusion.3
  77.1 4.0 %collective-permute-start.7 = (bf16[2,208,256]{2,1,0:T(8,128)(2,1)S(1)}, bf16[2,208,256]{2,1,0:T(8,128)(2,1)S(1)}, u32[]{:S(2)}, u32[]{:S(2)}) collective-permute-start(bf16[2,208,256]{2,1,0:T(8,128)(2,1)S(1)} %get-tuple-element.26), channel_id=1, source_target_pairs={{0,256},{256,512},{512,768},{768,0},{1,257},{257,513},{513,769},{7... | collective-permute-start | bytes 638984 | tf_op jit(solution)/shard_map/ppermute | solution.py:86
  81.1 3.6 %collective-permute-done.4 = bf16[2,208,256]{2,1,0:T(8,128)(2,1)} collective-permute-done((bf16[2,208,256]{2,1,0:T(8,128)(2,1)}, bf16[2,208,256]{2,1,0:T(8,128)(2,1)}, u32[]{:S(2)}, u32[]{:S(2)}) %collective-permute-start.4) | collective-permute-done | bytes 213024 | tf_op jit(solution)/shard_map/ppermute | solution.py:86
  84.7 10.9 %collective-permute-done.5 = bf16[2,208,256]{2,1,0:T(8,128)(2,1)} collective-permute-done((bf16[2,208,256]{2,1,0:T(8,128)(2,1)}, bf16[2,208,256]{2,1,0:T(8,128)(2,1)}, u32[]{:S(2)}, u32[]{:S(2)}) %collective-permute-start.5) | collective-permute-done | bytes 213024 | tf_op jit(solution)/shard_map/ppermute | solution.py:86
  95.7 0.0 copy-done.2
  95.7 0.0 collective-permute-done.6
  95.7 1.4 fusion.6
  97.0 2.6 %collective-permute-start.10 = (bf16[208,256]{1,0:T(8,128)(2,1)S(1)}, bf16[208,256]{1,0:T(8,128)(2,1)S(1)}, u32[]{:S(2)}, u32[]{:S(2)}) collective-permute-start(bf16[208,256]{1,0:T(8,128)(2,1)S(1)} %fusion.7), channel_id=1, source_target_pairs={{0,128},{128,0},{1,129},{129,1},{2,130},{130,2},{3,131},{131,3},{4... | collective-permute-start | bytes 319496 | tf_op jit(solution)/shard_map/ppermute | solution.py:102
  99.7 9.1 %collective-permute-start.8 = (bf16[2,208,256]{2,1,0:T(8,128)(2,1)S(1)}, bf16[2,208,256]{2,1,0:T(8,128)(2,1)S(1)}, u32[]{:S(2)}, u32[]{:S(2)}) collective-permute-start(bf16[2,208,256]{2,1,0:T(8,128)(2,1)S(1)} %get-tuple-element.24), channel_id=1, source_target_pairs={{0,512},{256,768},{512,0},{768,256},{1,513},{257,769},{513,1},{769... | collective-permute-start | bytes 638984 | tf_op jit(solution)/shard_map/ppermute | solution.py:86
  108.8 5.0 %collective-permute-start.9 = (bf16[2,208,256]{2,1,0:T(8,128)(2,1)S(1)}, bf16[2,208,256]{2,1,0:T(8,128)(2,1)S(1)}, u32[]{:S(2)}, u32[]{:S(2)}) collective-permute-start(bf16[2,208,256]{2,1,0:T(8,128)(2,1)S(1)} %get-tuple-element.25), channel_id=1, source_target_pairs={{0,768},{256,0},{512,256},{768,512},{1,769},{257,1},{513,257},{769... | collective-permute-start | bytes 638984 | tf_op jit(solution)/shard_map/ppermute | solution.py:86
  113.9 0.0 collective-permute-done.2
  113.9 0.0 copy-done.1
  113.9 2.1 %fusion = bf16[8,32,1024]{2,1,0:T(8,128)(2,1)} fusion(bf16[8,32,1024]{2,1,0:T(8,128)(2,1)} %collective-permute-done.2, bf16[8,2,32,1024]{3,2,1,0:T(8,128)(2,1)S(1)} %bitcast.73, s32[]{:T(128)S(6)} %select_n.131), kind=kLoop, calls=%fused_computation.7 | loop fusion | flops 1048576 | bytes 1572868 | tf_op jit(solution)/shard_map/convert_element_type | solution.py:91
  115.9 5.2 %all-to-all-start.2 = ((bf16[8,32,1024]{2,1,0:T(8,128)(2,1)}), bf16[8,32,1024]{2,1,0:T(8,128)(2,1)S(1)}, u32[]{:S(2)}, u32[]{:S(2)}) async-start(bf16[8,32,1024]{2,1,0:T(8,128)(2,1)} %fusion), calls=%async_computation.2 | async-start | bytes 1048576 | tf_op jit(solution)/shard_map/all_to_all | solution.py:92
  121.1 0.0 copy-start.4
  121.2 0.0 collective-permute-done.7
  121.2 0.0 collective-permute-done.8
  121.2 0.0 collective-permute-done.9
  121.2 1.1 fusion.4
  122.3 2.8 %collective-permute-start.11 = (bf16[208,256]{1,0:T(8,128)(2,1)S(1)}, bf16[208,256]{1,0:T(8,128)(2,1)S(1)}, u32[]{:S(2)}, u32[]{:S(2)}) collective-permute-start(bf16[208,256]{1,0:T(8,128)(2,1)S(1)} %fusion.8), channel_id=1, source_target_pairs={{0,128},{128,0},{1,129},{129,1},{2,130},{130,2},{3,131},{131,3},{4... | collective-permute-start | bytes 319496 | tf_op jit(solution)/shard_map/ppermute | solution.py:102
  125.1 0.0 collective-permute-done.10
  125.2 0.9 collective-permute-done.11
  126.0 0.1 convert_select_fusion.1
  126.2 0.0 copy-done.4
  126.2 2.3 %fusion.2 = (bf16[1,208,1024]{2,1,0:T(8,128)(2,1)}, f32[1,208,1024]{2,1,0:T(8,128)}) fusion(bf16[1664,1024]{1,0:T(8,128)(2,1)} %param.5, s32[]{:T(128)S(6)} %select_n.158, f32[208,512]{1,0:T(8,128)S(1)} %get-tuple-element.28, f32[208,512]{1,0:T(8,128)S(1)} %get-tuple-element.27, f32[1,208,1024]{2,1,0:T(8,128)S(1)} %copy-done.4), kind=kLoop, calls=%fused_computation.11 | loop fusion | flops 1490944 | bytes 3407876 | tf_op jit(solution)/shard_map/convert_element_type | solution.py:110
  128.5 10.6 %all-to-all-done.2 = bf16[8,32,1024]{2,1,0:T(8,128)(2,1)S(1)} async-done(((bf16[8,32,1024]{2,1,0:T(8,128)(2,1)}), bf16[8,32,1024]{2,1,0:T(8,128)(2,1)S(1)}, u32[]{:S(2)}, u32[]{:S(2)}) %all-to-all-start.2) | async-done | bytes 524320 | tf_op jit(solution)/shard_map/all_to_all | solution.py:92
  139.1 0.7 reduce_sum.12
  (9 shorter events, 0.1 us)
Async XLA Ops:
  1.4 16.8 %collective-permute-start = (bf16[32,256]{1,0:T(8,128)(2,1)S(1)}, bf16[32,256]{1,0:T(8,128)(2,1)S(1)}, u32[]{:S(2)}, u32[]{:S(2)}) collective-permute-start(bf16[32,256]{1,0:T(8,128)(2,1)S(1)} %constant_dynamic-slice_fusion), channel_id=1, source_target_pairs={{0,128},{128,0},{1,129},{129,1},{2,130},{130,2},{3,131},{131,3},{4... | collective-permute-start | bytes 49160 | tf_op jit(solution)/shard_map/ppermute | solution.py:46
  18.2 40.2 %collective-permute-start.3 = (bf16[512,1664]{1,0:T(8,128)(2,1)}, bf16[512,1664]{1,0:T(8,128)(2,1)S(1)}, u32[]{:S(2)}, u32[]{:S(2)}) collective-permute-start(bf16[512,1664]{1,0:T(8,128)(2,1)} %param.4), channel_id=1, source_target_pairs={{0,128},{128,0},{1,129},{129,1},{2,130},{130,2},{3,131},{131,3},{4... | collective-permute-start | bytes 5111816 | tf_op jit(solution)/shard_map/ppermute | solution.py:53
  22.2 29.4 %all-to-all-start = ((bf16[32,32,256]{2,1,0:T(8,128)(2,1)}), bf16[32,32,256]{2,1,0:T(8,128)(2,1)}, u32[]{:S(2)}, u32[]{:S(2)}) async-start(bf16[32,32,256]{2,1,0:T(8,128)(2,1)} %bitcast.12), calls=%async_computation | async-start | bytes 1048576 | tf_op jit(solution)/shard_map/all_to_all | solution.py:35
  34.4 24.1 %copy-start = (bf16[512,1664]{1,0:T(8,128)(2,1)S(1)}, bf16[512,1664]{1,0:T(8,128)(2,1)}, u32[]{:S(2)}) copy-start(bf16[512,1664]{1,0:T(8,128)(2,1)} %param.4) | copy-start | bytes 5111812
  35.2 14.4 %collective-permute-start.1 = (bf16[2,32,256]{2,1,0:T(8,128)(2,1)S(1)}, bf16[2,32,256]{2,1,0:T(8,128)(2,1)S(1)}, u32[]{:S(2)}, u32[]{:S(2)}) collective-permute-start(bf16[2,32,256]{2,1,0:T(8,128)(2,1)S(1)} %pad_maximum_fusion.4), channel_id=1, source_target_pairs={{0,8},{8,0},{1,9},{9,1},{2,10},{10,2},{3,11},{11,3},{4,12},{12,4},... | collective-permute-start | bytes 98312 | tf_op jit(solution)/shard_map/ppermute | solution.py:48
  49.6 64.2 %collective-permute-start.2 = (bf16[8,32,1024]{2,1,0:T(8,128)(2,1)}, bf16[8,32,1024]{2,1,0:T(8,128)(2,1)}, u32[]{:S(2)}, u32[]{:S(2)}) collective-permute-start(bf16[8,32,1024]{2,1,0:T(8,128)(2,1)} %dynamic-slice_bitcast_fusion), channel_id=1, source_target_pairs={{0,8},{8,0},{1,9},{9,1},{2,10},{10,2},{3,11},{11,3},{4,12},{12,4},... | collective-permute-start | bytes 1572872 | tf_op jit(solution)/shard_map/ppermute | solution.py:66
  52.4 22.4 %all-to-all-start.1 = ((bf16[8,2,2,32,256]{4,3,2,1,0:T(8,128)(2,1)}), bf16[8,2,2,32,256]{4,3,2,1,0:T(8,128)(2,1)}, u32[]{:S(2)}, u32[]{:S(2)}) async-start(bf16[8,2,2,32,256]{4,3,2,1,0:T(8,128)(2,1)} %broadcast_in_dim.21), calls=%async_computation.1 | async-start | bytes 1048576 | tf_op jit(solution)/shard_map/all_to_all | solution.py:51
  61.3 0.9 copy-start.3
  63.0 21.7 %collective-permute-start.4 = (bf16[2,208,256]{2,1,0:T(8,128)(2,1)}, bf16[2,208,256]{2,1,0:T(8,128)(2,1)}, u32[]{:S(2)}, u32[]{:S(2)}) collective-permute-start(bf16[2,208,256]{2,1,0:T(8,128)(2,1)} %get-tuple-element.23), channel_id=1, source_target_pairs={{0,256},{256,512},{512,768},{768,0},{1,257},{257,513},{513,769},{7... | collective-permute-start | bytes 638984 | tf_op jit(solution)/shard_map/ppermute | solution.py:86
  67.3 28.4 %collective-permute-start.5 = (bf16[2,208,256]{2,1,0:T(8,128)(2,1)}, bf16[2,208,256]{2,1,0:T(8,128)(2,1)}, u32[]{:S(2)}, u32[]{:S(2)}) collective-permute-start(bf16[2,208,256]{2,1,0:T(8,128)(2,1)} %get-tuple-element.22), channel_id=1, source_target_pairs={{0,512},{256,768},{512,0},{768,256},{1,513},{257,769},{513,1},{769... | collective-permute-start | bytes 638984 | tf_op jit(solution)/shard_map/ppermute | solution.py:86
  72.7 23.0 %collective-permute-start.6 = (bf16[2,208,256]{2,1,0:T(8,128)(2,1)}, bf16[2,208,256]{2,1,0:T(8,128)(2,1)}, u32[]{:S(2)}, u32[]{:S(2)}) collective-permute-start(bf16[2,208,256]{2,1,0:T(8,128)(2,1)} %get-tuple-element.21), channel_id=1, source_target_pairs={{0,768},{256,0},{512,256},{768,512},{1,769},{257,1},{513,257},{769... | collective-permute-start | bytes 638984 | tf_op jit(solution)/shard_map/ppermute | solution.py:86
  77.0 18.7 %copy-start.2 = (bf16[1664,256]{1,0:T(8,128)(2,1)}, bf16[1664,256]{1,0:T(8,128)(2,1)S(1)}, u32[]{:S(2)}) copy-start(bf16[1664,256]{1,0:T(8,128)(2,1)S(1)} %convolution_convert_fusion.1) | copy-start | bytes 2555908
  77.0 36.9 %copy-start.1 = (bf16[512,1024]{1,0:T(8,128)(2,1)S(1)}, bf16[512,1024]{1,0:T(8,128)(2,1)}, u32[]{:S(2)}) copy-start(bf16[512,1024]{1,0:T(8,128)(2,1)} %convolution_convert_fusion.2) | copy-start | bytes 3145732
  77.1 44.1 %collective-permute-start.7 = (bf16[2,208,256]{2,1,0:T(8,128)(2,1)S(1)}, bf16[2,208,256]{2,1,0:T(8,128)(2,1)S(1)}, u32[]{:S(2)}, u32[]{:S(2)}) collective-permute-start(bf16[2,208,256]{2,1,0:T(8,128)(2,1)S(1)} %get-tuple-element.26), channel_id=1, source_target_pairs={{0,256},{256,512},{512,768},{768,0},{1,257},{257,513},{513,769},{7... | collective-permute-start | bytes 638984 | tf_op jit(solution)/shard_map/ppermute | solution.py:86
  97.0 28.1 %collective-permute-start.10 = (bf16[208,256]{1,0:T(8,128)(2,1)S(1)}, bf16[208,256]{1,0:T(8,128)(2,1)S(1)}, u32[]{:S(2)}, u32[]{:S(2)}) collective-permute-start(bf16[208,256]{1,0:T(8,128)(2,1)S(1)} %fusion.7), channel_id=1, source_target_pairs={{0,128},{128,0},{1,129},{129,1},{2,130},{130,2},{3,131},{131,3},{4... | collective-permute-start | bytes 319496 | tf_op jit(solution)/shard_map/ppermute | solution.py:102
  99.7 21.5 %collective-permute-start.8 = (bf16[2,208,256]{2,1,0:T(8,128)(2,1)S(1)}, bf16[2,208,256]{2,1,0:T(8,128)(2,1)S(1)}, u32[]{:S(2)}, u32[]{:S(2)}) collective-permute-start(bf16[2,208,256]{2,1,0:T(8,128)(2,1)S(1)} %get-tuple-element.24), channel_id=1, source_target_pairs={{0,512},{256,768},{512,0},{768,256},{1,513},{257,769},{513,1},{769... | collective-permute-start | bytes 638984 | tf_op jit(solution)/shard_map/ppermute | solution.py:86
  108.8 12.4 %collective-permute-start.9 = (bf16[2,208,256]{2,1,0:T(8,128)(2,1)S(1)}, bf16[2,208,256]{2,1,0:T(8,128)(2,1)S(1)}, u32[]{:S(2)}, u32[]{:S(2)}) collective-permute-start(bf16[2,208,256]{2,1,0:T(8,128)(2,1)S(1)} %get-tuple-element.25), channel_id=1, source_target_pairs={{0,768},{256,0},{512,256},{768,512},{1,769},{257,1},{513,257},{769... | collective-permute-start | bytes 638984 | tf_op jit(solution)/shard_map/ppermute | solution.py:86
  115.9 23.2 %all-to-all-start.2 = ((bf16[8,32,1024]{2,1,0:T(8,128)(2,1)}), bf16[8,32,1024]{2,1,0:T(8,128)(2,1)S(1)}, u32[]{:S(2)}, u32[]{:S(2)}) async-start(bf16[8,32,1024]{2,1,0:T(8,128)(2,1)} %fusion), calls=%async_computation.2 | async-start | bytes 1048576 | tf_op jit(solution)/shard_map/all_to_all | solution.py:92
  121.1 5.0 %copy-start.4 = (f32[1,208,1024]{2,1,0:T(8,128)S(1)}, f32[1,208,1024]{2,1,0:T(8,128)}, u32[]{:S(2)}) copy-start(f32[1,208,1024]{2,1,0:T(8,128)} %param.7) | copy-start | bytes 2555908
  122.3 3.7 %collective-permute-start.11 = (bf16[208,256]{1,0:T(8,128)(2,1)S(1)}, bf16[208,256]{1,0:T(8,128)(2,1)S(1)}, u32[]{:S(2)}, u32[]{:S(2)}) collective-permute-start(bf16[208,256]{1,0:T(8,128)(2,1)S(1)} %fusion.8), channel_id=1, source_target_pairs={{0,128},{128,0},{1,129},{129,1},{2,130},{130,2},{3,131},{131,3},{4... | collective-permute-start | bytes 319496 | tf_op jit(solution)/shard_map/ppermute | solution.py:102
where the time goes:
time: 141 us; the launch traced here: 140 us
  starting transfers between devices  80.5 us (57%)
  waiting for transfers between devices  32.2 us (23%)
  matrix products  9.83 us (7%)
  other arithmetic  9.14 us (6%)
  local copies, waits for them, and re-layouts  7.12 us (5%)
    ppermute x6, starting transfers between devices, step(): lax.ppermute(s, 'z_lo', [(i, (i + d) % n_z) for i in range(n_z)])  30 us
    ppermute x1, starting transfers between devices, step(): partner = lax.ppermute(second_part(1 - core), 'core', SWAP)  16 us
    ppermute x6, waiting for transfers between devices, step(): lax.ppermute(s, 'z_lo', [(i, (i + d) % n_z) for i in range(n_z)])  14.5 us
    all_to_all x1, waiting for transfers between devices, step(): lax.all_to_all(paired, 'x', split_axis=0, concat_axis=0, tiled=True)  10.6 us
    ppermute x1, starting transfers between devices, step(): far_pair = lax.ppermute(pair, 'z_hi', SWAP)  7.17 us
    all_to_all x1, starting transfers between devices, step(): lax.all_to_all(sent.reshape(4 * n_x, own_tokens, part), ('x', 'core', 'z_...  6.59 us
    all_to_all x1, starting transfers between devices, step(): lax.all_to_all(after(sent, gathered0), 'x', split_axis=0, concat_axis=0,...  6 us
    dot_general x1, matrix products, step(): jnp.dot(activations, weight, preferred_element_type=jnp.float32)  5.55 us
  transfers between devices with their start and end apart: 15, of which 6 were waited for; matrix products, arithmetic and copies ran while one was open for 17% of the time, Pallas kernels for 0%

commit v1 on v0

v1 whole, which is shorter than its diff:
```python
import jax
import jax.numpy as jnp
import numpy as np
from jax import lax
from jax.sharding import Mesh, PartitionSpec as P


momentum_decay = 0.9
step_size = 0.05

SWAP = [(0, 1), (1, 0)]


def after(value, *others):
    return lax.optimization_barrier((value, *others))[0]


def placed(index, mine, other, axis, shape):
    return jnp.where(lax.broadcasted_iota(jnp.int32, shape, axis) == index, mine, other)


def halves(arrays, index):
    def entry(i):
        at = (lax.dynamic_index_in_dim(a, i, 0, keepdims=False) for a in arrays)
        return sum(a.astype(jnp.float32) for a in at)

    return lax.optimization_barrier((entry(index), entry(1 - index).astype(jnp.bfloat16)))


def step(activations, weight, out_grad, momentum):
    slab_rows = momentum.shape[1]
    tokens, hid = activations.shape
    own_tokens, cols = out_grad.shape
    n_x = tokens // own_tokens // 2
    half = cols // 2
    part = half // 2
    core, z_hi, z_lo = (lax.axis_index(a) for a in ("core", "z_hi", "z_lo"))

    mine = lax.dynamic_slice_in_dim(out_grad, core * half, half, 1)
    other = lax.dynamic_slice_in_dim(out_grad, (1 - core) * half, half, 1)
    partner = lax.ppermute(other, "core", SWAP)
    pair = placed(core, mine, partner, 0, (2, own_tokens, half))
    far = lax.ppermute(pair, "z_hi", SWAP)
    shape = (n_x, 2, 2, own_tokens, part)
    gathered = []
    for p in range(2):
        near_p, far_p = (a[None, :, None, :, p * part : (p + 1) * part] for a in (pair, far))
        sent = placed(z_hi, near_p, far_p, 2, shape)
        if p == 0:
            pair, far = lax.optimization_barrier((pair, far, sent))[:2]
        else:
            sent = after(sent, gathered[0])
        gathered.append(lax.all_to_all(sent, "x", split_axis=0, concat_axis=0, tiled=True))

    partner_act = lax.ppermute(activations, "core", SWAP)
    both_act = placed(
        core,
        activations.reshape(n_x, 1, 2 * own_tokens, hid),
        partner_act.reshape(n_x, 1, 2 * own_tokens, hid),
        1,
        (n_x, 2, 2 * own_tokens, hid),
    ).reshape(2 * tokens, hid)
    both_act = lax.optimization_barrier(both_act)

    partial_out = jnp.dot(activations, weight, preferred_element_type=jnp.float32)
    partial_out = partial_out.astype(jnp.bfloat16).reshape(n_x, 2, own_tokens, cols)
    keep_out = lax.dynamic_index_in_dim(partial_out, z_hi, 1, keepdims=False)
    give_out = lax.dynamic_index_in_dim(partial_out, 1 - z_hi, 1, keepdims=False)
    got_out = lax.ppermute(after(give_out, far), "z_hi", SWAP)

    def product(rows):
        local_grad = lax.dot_general(
            both_act,
            rows.reshape(2 * tokens, part),
            (((0,), (0,)), ((), ())),
            preferred_element_type=jnp.float32,
        )
        return local_grad.astype(jnp.bfloat16)

    bits = (z_lo // 2, z_lo % 2)
    slabs = product(gathered[0]).reshape(2, 2, 2, slab_rows, part)
    keep = lax.dynamic_index_in_dim(slabs, bits[1], 1, keepdims=False)
    give = lax.dynamic_index_in_dim(slabs, 1 - bits[1], 1, keepdims=False)
    keep, give = lax.optimization_barrier((keep, give))
    got = lax.ppermute(give, "z_lo", [(i, i ^ 1) for i in range(4)])
    slabs = product(after(gathered[1], give)).reshape(4, 2, slab_rows, part)
    keep, give = halves((keep, got), bits[0])
    got = lax.ppermute(give, "z_lo", [(i, i ^ 2) for i in range(4)])
    pieces = lax.optimization_barrier(
        tuple(lax.dynamic_index_in_dim(slabs, (z_lo + d) % 4, 0, keepdims=False) for d in range(4))
    )
    arrived = [
        lax.ppermute(pieces[d], "z_lo", [(i, (i + d) % 4) for i in range(4)]) for d in (1, 2, 3)
    ]
    own_part, got_part = [], []
    keep, give = halves((keep, got), core)
    own_part.append(keep)
    got_part.append(give)
    keep, give = halves((after(pieces[0], give), *arrived), core)
    own_part.append(keep)
    got_part.append(give)
    got = lax.ppermute(jnp.concatenate(got_part, axis=1), "core", SWAP).astype(jnp.float32)
    own = jnp.concatenate(own_part, axis=1)

    paired = (keep_out.astype(jnp.float32) + got_out.astype(jnp.float32)).astype(jnp.bfloat16)
    pieces = lax.all_to_all(
        after(paired, gathered[1]), "x", split_axis=0, concat_axis=0, tiled=True
    )
    summed = jnp.sum(pieces.astype(jnp.float32), axis=0).astype(jnp.bfloat16)

    grad_share = jnp.concatenate(
        [jnp.where(core == 0, own, got), jnp.where(core == 0, got, own)], axis=1
    )
    new_momentum = momentum_decay * momentum + grad_share[None]
    own_rows = lax.dynamic_slice_in_dim(weight, (z_lo * 2 + core) * slab_rows, slab_rows, 0)
    new_weight = (own_rows.astype(jnp.float32)[None] - step_size * new_momentum).astype(
        jnp.bfloat16
    )
    return (summed, new_momentum, new_weight)


def solution(mesh):
    n_dp, n_hidden, n_mp = (mesh.shape[a] for a in ("dp", "hidden", "mp"))
    grid = np.asarray(mesh.devices).reshape(n_dp // 2, 2, n_hidden // 2, 2, n_mp)
    finer = Mesh(grid, ("z_lo", "core", "x", "z_hi", "mp"))
    dp, hidden = ("z_lo", "core"), ("x", "z_hi")
    return jax.shard_map(
        step,
        mesh=finer,
        in_specs=(P(dp, hidden), P(hidden, "mp"), P(dp + hidden, "mp"), P(dp, hidden, "mp")),
        out_specs=(P(dp + hidden, "mp"), P(dp, hidden, "mp"), P(dp, hidden, "mp")),
        check_vma=False,
    )
```

time: 141 us -> 140 us (level)
  starting transfers between devices: 80.5 us -> 66.5 us
  waiting for transfers between devices: 32.2 us -> 44.9 us
  other arithmetic: 9.14 us -> 11.7 us
  local copies, waits for them, and re-layouts: 7.12 us -> 5.26 us
    ppermute x12 -> x10, starting transfers between devices: 62.7 us -> 51.7 us  [the longest x1 16 us: step(): partner = lax.ppermute(other, 'core', SWAP)]
    all_to_all x3, waiting for transfers between devices: 10.6 us -> 20.7 us  [the longest x2 13.6 us: step(): lax.all_to_all(sent, 'x', split_axis=0, concat_axis=0, tiled=True)]
    select_n x2 -> x5, other arithmetic: 0.41 us -> 4.35 us  [the longest x4 4.26 us: placed(): jnp.where(lax.broadcasted_iota(jnp.int32, shape, axis) == index, mine, ot...]
    all_to_all x3, starting transfers between devices: 17.8 us -> 14.8 us  [the longest x2 8.28 us: step(): lax.all_to_all(sent, 'x', split_axis=0, concat_axis=0, tiled=True)]
    ppermute x12 -> x10, waiting for transfers between devices: 21.6 us -> 24.2 us  [the longest x1 12.6 us: step(): got = lax.ppermute(give, 'z_lo', [(i, i ^ 1) for i in range(4)])]
    add x2 -> x1, other arithmetic: 2.45 us -> 0.13 us  [entry(): return sum((a.astype(jnp.float32) for a in at))]
    convert_element_type x1 -> x3, other arithmetic: 2.06 us -> 4.17 us  [the longest x2 2.13 us: halves(): entry(1 - index).astype(jnp.bfloat16)]
    broadcast_in_dim x2 -> x0, local copies, waits for them, and re-layouts: 1.71 us -> none  [the longest x1 0.85 us: step(): sent = jnp.broadcast_to(sent[None, :, None], (n_x, 2, 2, own_tokens, part))]
  transfers between devices with their start and end apart: 15 -> 13, of which waited for: 6 -> 6; matrix products, arithmetic and copies ran while one was open for 17% -> 17% of each run, Pallas kernels for 0% -> 0%
where the time goes in v1:
time: 140 us; the launch traced here: 139 us
  starting transfers between devices  66.5 us (48%)
  waiting for transfers between devices  44.9 us (32%)
  other arithmetic  11.7 us (8%)
  matrix products  9.36 us (7%)
  local copies, waits for them, and re-layouts  5.26 us (4%)
    ppermute x1, starting transfers between devices, step(): partner = lax.ppermute(other, 'core', SWAP)  16 us
    all_to_all x2, waiting for transfers between devices, step(): lax.all_to_all(sent, 'x', split_axis=0, concat_axis=0, tiled=True)  13.6 us
    ppermute x1, waiting for transfers between devices, step(): got = lax.ppermute(give, 'z_lo', [(i, i ^ 1) for i in range(4)])  12.6 us
    ppermute x3, starting transfers between devices, step(): lax.ppermute(pieces[d], 'z_lo', [(i, (i + d) % 4) for i in range(4)])  11.2 us
    ppermute x1, starting transfers between devices, step(): got = lax.ppermute(give, 'z_lo', [(i, i ^ 2) for i in range(4)])  8.67 us
    all_to_all x2, starting transfers between devices, step(): lax.all_to_all(sent, 'x', split_axis=0, concat_axis=0, tiled=True)  8.28 us
    all_to_all x1, waiting for transfers between devices, step(): lax.all_to_all(after(paired, gathered[1]), 'x', split_axis=0, concat_axis...  7.17 us
    ppermute x1, waiting for transfers between devices, step(): far = lax.ppermute(pair, 'z_hi', SWAP)  6.96 us
  transfers between devices with their start and end apart: 13, of which 6 were waited for; matrix products, arithmetic and copies ran while one was open for 17% of the time, Pallas kernels for 0%

profile of v1, /device:TPU:1, one launch (start us, length us, event | category | flops | bytes accessed | tf_op | source)
XLA Modules:
  0.0 138.7 jit_solution(5605570294701991374)
XLA Ops:
  0.6 0.0 copy-start
  0.6 0.9 constant_dynamic-slice_fusion.1
  1.6 16.0 %collective-permute-start = (bf16[32,512]{1,0:T(8,128)(2,1)S(1)}, bf16[32,512]{1,0:T(8,128)(2,1)S(1)}, u32[]{:S(2)}, u32[]{:S(2)}) collective-permute-start(bf16[32,512]{1,0:T(8,128)(2,1)S(1)} %get-tuple-element.58), channel_id=1, source_target_pairs={{0,128},{128,0},{1,129},{129,1},{2,130},{130,2},{3,131},{131,3},{4... | collective-permute-start | bytes 98312 | tf_op jit(solution)/shard_map/ppermute | solution.py:41
  17.6 1.9 %collective-permute-start.3 = (bf16[512,1664]{1,0:T(8,128)(2,1)}, bf16[512,1664]{1,0:T(8,128)(2,1)S(1)}, u32[]{:S(2)}, u32[]{:S(2)}) collective-permute-start(bf16[512,1664]{1,0:T(8,128)(2,1)} %param.4), channel_id=1, source_target_pairs={{0,128},{128,0},{1,129},{129,1},{2,130},{130,2},{3,131},{131,3},{4... | collective-permute-start | bytes 5111816 | tf_op jit(solution)/shard_map/ppermute | solution.py:55
  19.5 0.0 collective-permute-done
  19.5 0.1 broadcast_select_fusion.2
  19.6 1.9 %collective-permute-start.1 = (bf16[2,32,512]{2,1,0:T(8,128)(2,1)S(1)}, bf16[2,32,512]{2,1,0:T(8,128)(2,1)S(1)}, u32[]{:S(2)}, u32[]{:S(2)}) collective-permute-start(bf16[2,32,512]{2,1,0:T(8,128)(2,1)S(1)} %broadcast_select_fusion.2), channel_id=1, source_target_pairs={{0,8},{8,0},{1,9},{9,1},{2,10},{10,2},{3,11},{11,3},{4,12},{12,4},... | collective-permute-start | bytes 196616 | tf_op jit(solution)/shard_map/ppermute | solution.py:43
  21.6 7.0 %collective-permute-done.1 = bf16[2,32,512]{2,1,0:T(8,128)(2,1)S(1)} collective-permute-done((bf16[2,32,512]{2,1,0:T(8,128)(2,1)S(1)}, bf16[2,32,512]{2,1,0:T(8,128)(2,1)S(1)}, u32[]{:S(2)}, u32[]{:S(2)}) %collective-permute-start.1) | collective-permute-done | bytes 65568 | tf_op jit(solution)/shard_map/ppermute | solution.py:43
  28.5 0.9 broadcast_select_fusion.1
  29.4 4.1 %all-to-all-start = ((bf16[8,2,2,32,256]{4,3,2,1,0:T(8,128)(2,1)}), bf16[8,2,2,32,256]{4,3,2,1,0:T(8,128)(2,1)}, u32[]{:S(2)}, u32[]{:S(2)}) async-start(bf16[8,2,2,32,256]{4,3,2,1,0:T(8,128)(2,1)} %broadcast_select_fusion.1), calls=%async_computation | async-start | bytes 1048576 | tf_op jit(solution)/shard_map/all_to_all | solution.py:53
  33.6 0.9 broadcast_select_fusion
  34.5 13.6 %all-to-all-done = bf16[8,2,2,32,256]{4,3,2,1,0:T(8,128)(2,1)} async-done(((bf16[8,2,2,32,256]{4,3,2,1,0:T(8,128)(2,1)}), bf16[8,2,2,32,256]{4,3,2,1,0:T(8,128)(2,1)}, u32[]{:S(2)}, u32[]{:S(2)}) %all-to-all-start) | async-done | bytes 524320 | tf_op jit(solution)/shard_map/all_to_all | solution.py:53
  48.1 4.1 %all-to-all-start.1 = ((bf16[8,2,2,32,256]{4,3,2,1,0:T(8,128)(2,1)}), bf16[8,2,2,32,256]{4,3,2,1,0:T(8,128)(2,1)}, u32[]{:S(2)}, u32[]{:S(2)}) async-start(bf16[8,2,2,32,256]{4,3,2,1,0:T(8,128)(2,1)} %broadcast_select_fusion), calls=%async_computation.1 | async-start | bytes 1048576 | tf_op jit(solution)/shard_map/all_to_all | solution.py:53
  52.2 0.0 copy-done
  52.2 5.0 %convolution_convert_fusion.2 = bf16[512,1024]{1,0:T(8,128)(2,1)} fusion(bf16[512,1664]{1,0:T(8,128)(2,1)S(1)} %copy-done, bf16[1664,1024]{1,0:T(8,128)(2,1)} %param.5), kind=kOutput, calls=%fused_computation.3 | convolution fusion | flops 1745354752 | bytes 6160384 | tf_op jit(solution)/shard_map/dot_general | solution.py:65
  57.2 0.1 iota.26
  57.3 0.1 iota.27
  57.4 1.9 %dynamic-slice_bitcast_fusion = bf16[8,32,1024]{2,1,0:T(8,128)(2,1)} fusion(bf16[8,2,32,1024]{3,2,1,0:T(8,128)(2,1)} %bitcast.56, s32[]{:T(128)S(6)} %select_n.119), kind=kLoop, calls=%fused_computation.12 | loop fusion | bytes 1048580 | tf_op jit(solution)/shard_map/jit(dynamic_index_in_dim)/squeeze | solution.py:68
  59.3 5.5 %collective-permute-start.2 = (bf16[8,32,1024]{2,1,0:T(8,128)(2,1)}, bf16[8,32,1024]{2,1,0:T(8,128)(2,1)}, u32[]{:S(2)}, u32[]{:S(2)}) collective-permute-start(bf16[8,32,1024]{2,1,0:T(8,128)(2,1)} %dynamic-slice_bitcast_fusion), channel_id=1, source_target_pairs={{0,8},{8,0},{1,9},{9,1},{2,10},{10,2},{3,11},{11,3},{4,12},{12,4},... | collective-permute-start | bytes 1572872 | tf_op jit(solution)/shard_map/ppermute | solution.py:69
  64.8 0.0 collective-permute-done.3
  64.8 0.0 copy-start.1
  64.8 1.2 copy-done.1
  66.0 2.4 %bitcast_select_fusion = bf16[1024,1664]{1,0:T(8,128)(2,1)S(1)} fusion(pred[1024]{0:T(1024)(128)(4,1)S(1)} %iota.27, bf16[8,64,1664]{2,1,0:T(8,128)(2,1)} %bitcast.55, bf16[8,64,1664]{2,1,0:T(8,128)(2,1)} %bitcast.54), kind=kLoop, calls=%fused_computation | loop fusion | flops 1703936 | bytes 6816768 | tf_op jit(solution)/shard_map/jit(_where)/select_n | solution.py:19
  68.4 2.1 %convolution_convert_fusion.1 = bf16[1664,256]{1,0:T(8,128)(2,1)S(1)} fusion(bf16[1024,1664]{1,0:T(8,128)(2,1)S(1)} %bitcast_select_fusion, bf16[1024,256]{1,0:T(8,128)(2,1)} %bitcast.7), kind=kOutput, calls=%fused_computation.2 | convolution fusion | flops 872841216 | bytes 4784128 | tf_op jit(solution)/shard_map/dot_general | solution.py:72
  70.6 1.0 dynamic-slice_bitcast_fusion.1
  71.5 4.0 %collective-permute-start.4 = (bf16[2,2,208,256]{3,2,1,0:T(8,128)(2,1)}, bf16[2,2,208,256]{3,2,1,0:T(8,128)(2,1)}, u32[]{:S(2)}, u32[]{:S(2)}) collective-permute-start(bf16[2,2,208,256]{3,2,1,0:T(8,128)(2,1)} %get-tuple-element.28), channel_id=1, source_target_pairs={{0,256},{256,0},{512,768},{768,512},{1,257},{257,1},{513,769},{769... | collective-permute-start | bytes 1277960 | tf_op jit(solution)/shard_map/ppermute | solution.py:85
  75.5 0.0 all-to-all-done.1
  75.6 0.0 copy-start.2
  75.6 2.2 %convolution_convert_fusion = bf16[1664,256]{1,0:T(8,128)(2,1)S(1)} fusion(bf16[1024,1664]{1,0:T(8,128)(2,1)S(1)} %bitcast_select_fusion, bf16[1024,256]{1,0:T(8,128)(2,1)} %bitcast.15), kind=kOutput, calls=%fused_computation.1 | convolution fusion | flops 872841216 | bytes 4784128 | tf_op jit(solution)/shard_map/dot_general | solution.py:72
  77.8 0.0 copy-start.3
  77.8 0.1 dynamic-slice_bitcast_fusion.3
  77.8 5.7 %collective-permute-start.8 = (bf16[2,208,256]{2,1,0:T(8,128)(2,1)S(1)}, bf16[2,208,256]{2,1,0:T(8,128)(2,1)S(1)}, u32[]{:S(2)}, u32[]{:S(2)}) collective-permute-start(bf16[2,208,256]{2,1,0:T(8,128)(2,1)S(1)} %get-tuple-element.38), channel_id=1, source_target_pairs={{0,768},{256,0},{512,256},{768,512},{1,769},{257,1},{513,257},{769... | collective-permute-start | bytes 638984 | tf_op jit(solution)/shard_map/ppermute | solution.py:93
  83.5 2.2 %collective-permute-start.7 = (bf16[2,208,256]{2,1,0:T(8,128)(2,1)S(1)}, bf16[2,208,256]{2,1,0:T(8,128)(2,1)S(1)}, u32[]{:S(2)}, u32[]{:S(2)}) collective-permute-start(bf16[2,208,256]{2,1,0:T(8,128)(2,1)S(1)} %get-tuple-element.37), channel_id=1, source_target_pairs={{0,512},{256,768},{512,0},{768,256},{1,513},{257,769},{513,1},{769... | collective-permute-start | bytes 638984 | tf_op jit(solution)/shard_map/ppermute | solution.py:93
  85.7 3.4 %collective-permute-start.6 = (bf16[2,208,256]{2,1,0:T(8,128)(2,1)S(1)}, bf16[2,208,256]{2,1,0:T(8,128)(2,1)S(1)}, u32[]{:S(2)}, u32[]{:S(2)}) collective-permute-start(bf16[2,208,256]{2,1,0:T(8,128)(2,1)S(1)} %get-tuple-element.36), channel_id=1, source_target_pairs={{0,256},{256,512},{512,768},{768,0},{1,257},{257,513},{513,769},{7... | collective-permute-start | bytes 638984 | tf_op jit(solution)/shard_map/ppermute | solution.py:93
  89.1 12.6 %collective-permute-done.4 = bf16[2,2,208,256]{3,2,1,0:T(8,128)(2,1)} collective-permute-done((bf16[2,2,208,256]{3,2,1,0:T(8,128)(2,1)}, bf16[2,2,208,256]{3,2,1,0:T(8,128)(2,1)}, u32[]{:S(2)}, u32[]{:S(2)}) %collective-permute-start.4) | collective-permute-done | bytes 426016 | tf_op jit(solution)/shard_map/ppermute | solution.py:85
  101.7 0.0 copy-done.2
  101.7 1.1 fusion.3
  102.8 0.0 copy-start.4
  102.8 8.7 %collective-permute-start.5 = (bf16[2,208,256]{2,1,0:T(8,128)(2,1)S(1)}, bf16[2,208,256]{2,1,0:T(8,128)(2,1)}, u32[]{:S(2)}, u32[]{:S(2)}) collective-permute-start(bf16[2,208,256]{2,1,0:T(8,128)(2,1)S(1)} %get-tuple-element.30), channel_id=1, source_target_pairs={{0,512},{256,768},{512,0},{768,256},{1,513},{257,769},{513,1},{769... | collective-permute-start | bytes 638984 | tf_op jit(solution)/shard_map/ppermute | solution.py:88
  111.5 0.0 collective-permute-done.2
  111.5 0.0 copy-done.3
  111.5 2.0 %fusion = bf16[8,32,1024]{2,1,0:T(8,128)(2,1)} fusion(bf16[8,32,1024]{2,1,0:T(8,128)(2,1)} %collective-permute-done.2, bf16[8,2,32,1024]{3,2,1,0:T(8,128)(2,1)S(1)} %bitcast.57, s32[]{:T(128)S(6)} %select_n.118), kind=kLoop, calls=%fused_computation.5 | loop fusion | flops 1048576 | bytes 1572868 | tf_op jit(solution)/shard_map/convert_element_type | solution.py:105
  113.6 6.5 %all-to-all-start.2 = ((bf16[8,32,1024]{2,1,0:T(8,128)(2,1)}), bf16[8,32,1024]{2,1,0:T(8,128)(2,1)S(1)}, u32[]{:S(2)}, u32[]{:S(2)}) async-start(bf16[8,32,1024]{2,1,0:T(8,128)(2,1)} %fusion), calls=%async_computation.2 | async-start | bytes 1048576 | tf_op jit(solution)/shard_map/all_to_all | solution.py:106
  120.1 3.6 %collective-permute-done.5 = bf16[2,208,256]{2,1,0:T(8,128)(2,1)} collective-permute-done((bf16[2,208,256]{2,1,0:T(8,128)(2,1)S(1)}, bf16[2,208,256]{2,1,0:T(8,128)(2,1)}, u32[]{:S(2)}, u32[]{:S(2)}) %collective-permute-start.5) | collective-permute-done | bytes 213024 | tf_op jit(solution)/shard_map/ppermute | solution.py:88
  123.7 1.0 fusion.4
  124.7 0.0 collective-permute-done.8
  124.7 0.0 collective-permute-done.7
  124.8 0.0 collective-permute-done.6
  124.8 0.1 fusion.5
  124.9 2.4 %collective-permute-start.9 = (bf16[208,512]{1,0:T(8,128)(2,1)S(1)}, bf16[208,512]{1,0:T(8,128)(2,1)S(1)}, u32[]{:S(2)}, u32[]{:S(2)}) collective-permute-start(bf16[208,512]{1,0:T(8,128)(2,1)S(1)} %pad_maximum_fusion), channel_id=1, source_target_pairs={{0,128},{128,0},{1,129},{129,1},{2,130},{130,2},{3,131},{131,3},{4... | collective-permute-start | bytes 638984 | tf_op jit(solution)/shard_map/ppermute | solution.py:102
  127.4 1.0 collective-permute-done.9
  128.4 0.1 convert_select_fusion.1
  128.5 0.0 copy-done.4
  128.5 2.3 %fusion.2 = (bf16[1,208,1024]{2,1,0:T(8,128)(2,1)}, f32[1,208,1024]{2,1,0:T(8,128)}) fusion(bf16[1664,1024]{1,0:T(8,128)(2,1)} %param.5, s32[]{:T(128)S(6)} %select_n.145, f32[208,512]{1,0:T(8,128)S(1)} %get-tuple-element.54, f32[208,512]{1,0:T(8,128)S(1)} %get-tuple-element.53, f32[1,208,1024]{2,1,0:T(8,128)S(1)} %copy-done.4), kind=kLoop, calls=%fused_computation.9 | loop fusion | flops 1490944 | bytes 3407876 | tf_op jit(solution)/shard_map/convert_element_type | solution.py:116
  130.8 7.2 %all-to-all-done.2 = bf16[8,32,1024]{2,1,0:T(8,128)(2,1)S(1)} async-done(((bf16[8,32,1024]{2,1,0:T(8,128)(2,1)}), bf16[8,32,1024]{2,1,0:T(8,128)(2,1)S(1)}, u32[]{:S(2)}, u32[]{:S(2)}) %all-to-all-start.2) | async-done | bytes 524320 | tf_op jit(solution)/shard_map/all_to_all | solution.py:106
  138.0 0.7 reduce_sum.12
  (9 shorter events, 0.1 us)
Async XLA Ops:
  0.6 51.6 %copy-start = (bf16[512,1664]{1,0:T(8,128)(2,1)S(1)}, bf16[512,1664]{1,0:T(8,128)(2,1)}, u32[]{:S(2)}) copy-start(bf16[512,1664]{1,0:T(8,128)(2,1)} %param.4) | copy-start | bytes 5111812
  1.6 18.0 %collective-permute-start = (bf16[32,512]{1,0:T(8,128)(2,1)S(1)}, bf16[32,512]{1,0:T(8,128)(2,1)S(1)}, u32[]{:S(2)}, u32[]{:S(2)}) collective-permute-start(bf16[32,512]{1,0:T(8,128)(2,1)S(1)} %get-tuple-element.58), channel_id=1, source_target_pairs={{0,128},{128,0},{1,129},{129,1},{2,130},{130,2},{3,131},{131,3},{4... | collective-permute-start | bytes 98312 | tf_op jit(solution)/shard_map/ppermute | solution.py:41
  17.6 47.2 %collective-permute-start.3 = (bf16[512,1664]{1,0:T(8,128)(2,1)}, bf16[512,1664]{1,0:T(8,128)(2,1)S(1)}, u32[]{:S(2)}, u32[]{:S(2)}) collective-permute-start(bf16[512,1664]{1,0:T(8,128)(2,1)} %param.4), channel_id=1, source_target_pairs={{0,128},{128,0},{1,129},{129,1},{2,130},{130,2},{3,131},{131,3},{4... | collective-permute-start | bytes 5111816 | tf_op jit(solution)/shard_map/ppermute | solution.py:55
  19.6 8.9 %collective-permute-start.1 = (bf16[2,32,512]{2,1,0:T(8,128)(2,1)S(1)}, bf16[2,32,512]{2,1,0:T(8,128)(2,1)S(1)}, u32[]{:S(2)}, u32[]{:S(2)}) collective-permute-start(bf16[2,32,512]{2,1,0:T(8,128)(2,1)S(1)} %broadcast_select_fusion.2), channel_id=1, source_target_pairs={{0,8},{8,0},{1,9},{9,1},{2,10},{10,2},{3,11},{11,3},{4,12},{12,4},... | collective-permute-start | bytes 196616 | tf_op jit(solution)/shard_map/ppermute | solution.py:43
  29.4 18.6 %all-to-all-start = ((bf16[8,2,2,32,256]{4,3,2,1,0:T(8,128)(2,1)}), bf16[8,2,2,32,256]{4,3,2,1,0:T(8,128)(2,1)}, u32[]{:S(2)}, u32[]{:S(2)}) async-start(bf16[8,2,2,32,256]{4,3,2,1,0:T(8,128)(2,1)} %broadcast_select_fusion.1), calls=%async_computation | async-start | bytes 1048576 | tf_op jit(solution)/shard_map/all_to_all | solution.py:53
  48.1 27.5 %all-to-all-start.1 = ((bf16[8,2,2,32,256]{4,3,2,1,0:T(8,128)(2,1)}), bf16[8,2,2,32,256]{4,3,2,1,0:T(8,128)(2,1)}, u32[]{:S(2)}, u32[]{:S(2)}) async-start(bf16[8,2,2,32,256]{4,3,2,1,0:T(8,128)(2,1)} %broadcast_select_fusion), calls=%async_computation.1 | async-start | bytes 1048576 | tf_op jit(solution)/shard_map/all_to_all | solution.py:53
  59.3 52.2 %collective-permute-start.2 = (bf16[8,32,1024]{2,1,0:T(8,128)(2,1)}, bf16[8,32,1024]{2,1,0:T(8,128)(2,1)}, u32[]{:S(2)}, u32[]{:S(2)}) collective-permute-start(bf16[8,32,1024]{2,1,0:T(8,128)(2,1)} %dynamic-slice_bitcast_fusion), channel_id=1, source_target_pairs={{0,8},{8,0},{1,9},{9,1},{2,10},{10,2},{3,11},{11,3},{4,12},{12,4},... | collective-permute-start | bytes 1572872 | tf_op jit(solution)/shard_map/ppermute | solution.py:69
  64.8 1.2 copy-start.1
  71.5 30.2 %collective-permute-start.4 = (bf16[2,2,208,256]{3,2,1,0:T(8,128)(2,1)}, bf16[2,2,208,256]{3,2,1,0:T(8,128)(2,1)}, u32[]{:S(2)}, u32[]{:S(2)}) collective-permute-start(bf16[2,2,208,256]{3,2,1,0:T(8,128)(2,1)} %get-tuple-element.28), channel_id=1, source_target_pairs={{0,256},{256,0},{512,768},{768,512},{1,257},{257,1},{513,769},{769... | collective-permute-start | bytes 1277960 | tf_op jit(solution)/shard_map/ppermute | solution.py:85
  75.6 26.1 %copy-start.2 = (bf16[2,2,208,256]{3,2,1,0:T(8,128)(2,1)S(1)}, bf16[2,2,208,256]{3,2,1,0:T(8,128)(2,1)}, u32[]{:S(2)}) copy-start(bf16[2,2,208,256]{3,2,1,0:T(8,128)(2,1)} %get-tuple-element.27) | copy-start | bytes 1277956
  77.8 33.8 %copy-start.3 = (bf16[512,1024]{1,0:T(8,128)(2,1)S(1)}, bf16[512,1024]{1,0:T(8,128)(2,1)}, u32[]{:S(2)}) copy-start(bf16[512,1024]{1,0:T(8,128)(2,1)} %convolution_convert_fusion.2) | copy-start | bytes 3145732
  77.8 46.9 %collective-permute-start.8 = (bf16[2,208,256]{2,1,0:T(8,128)(2,1)S(1)}, bf16[2,208,256]{2,1,0:T(8,128)(2,1)S(1)}, u32[]{:S(2)}, u32[]{:S(2)}) collective-permute-start(bf16[2,208,256]{2,1,0:T(8,128)(2,1)S(1)} %get-tuple-element.38), channel_id=1, source_target_pairs={{0,768},{256,0},{512,256},{768,512},{1,769},{257,1},{513,257},{769... | collective-permute-start | bytes 638984 | tf_op jit(solution)/shard_map/ppermute | solution.py:93
  83.5 41.2 %collective-permute-start.7 = (bf16[2,208,256]{2,1,0:T(8,128)(2,1)S(1)}, bf16[2,208,256]{2,1,0:T(8,128)(2,1)S(1)}, u32[]{:S(2)}, u32[]{:S(2)}) collective-permute-start(bf16[2,208,256]{2,1,0:T(8,128)(2,1)S(1)} %get-tuple-element.37), channel_id=1, source_target_pairs={{0,512},{256,768},{512,0},{768,256},{1,513},{257,769},{513,1},{769... | collective-permute-start | bytes 638984 | tf_op jit(solution)/shard_map/ppermute | solution.py:93
  85.7 39.0 %collective-permute-start.6 = (bf16[2,208,256]{2,1,0:T(8,128)(2,1)S(1)}, bf16[2,208,256]{2,1,0:T(8,128)(2,1)S(1)}, u32[]{:S(2)}, u32[]{:S(2)}) collective-permute-start(bf16[2,208,256]{2,1,0:T(8,128)(2,1)S(1)} %get-tuple-element.36), channel_id=1, source_target_pairs={{0,256},{256,512},{512,768},{768,0},{1,257},{257,513},{513,769},{7... | collective-permute-start | bytes 638984 | tf_op jit(solution)/shard_map/ppermute | solution.py:93
  102.8 25.7 %copy-start.4 = (f32[1,208,1024]{2,1,0:T(8,128)S(1)}, f32[1,208,1024]{2,1,0:T(8,128)}, u32[]{:S(2)}) copy-start(f32[1,208,1024]{2,1,0:T(8,128)} %param.7) | copy-start | bytes 2555908
  102.8 20.9 %collective-permute-start.5 = (bf16[2,208,256]{2,1,0:T(8,128)(2,1)S(1)}, bf16[2,208,256]{2,1,0:T(8,128)(2,1)}, u32[]{:S(2)}, u32[]{:S(2)}) collective-permute-start(bf16[2,208,256]{2,1,0:T(8,128)(2,1)S(1)} %get-tuple-element.30), channel_id=1, source_target_pairs={{0,512},{256,768},{512,0},{768,256},{1,513},{257,769},{513,1},{769... | collective-permute-start | bytes 638984 | tf_op jit(solution)/shard_map/ppermute | solution.py:88
  113.6 24.4 %all-to-all-start.2 = ((bf16[8,32,1024]{2,1,0:T(8,128)(2,1)}), bf16[8,32,1024]{2,1,0:T(8,128)(2,1)S(1)}, u32[]{:S(2)}, u32[]{:S(2)}) async-start(bf16[8,32,1024]{2,1,0:T(8,128)(2,1)} %fusion), calls=%async_computation.2 | async-start | bytes 1048576 | tf_op jit(solution)/shard_map/all_to_all | solution.py:106
  124.9 3.5 %collective-permute-start.9 = (bf16[208,512]{1,0:T(8,128)(2,1)S(1)}, bf16[208,512]{1,0:T(8,128)(2,1)S(1)}, u32[]{:S(2)}, u32[]{:S(2)}) collective-permute-start(bf16[208,512]{1,0:T(8,128)(2,1)S(1)} %pad_maximum_fusion), channel_id=1, source_target_pairs={{0,128},{128,0},{1,129},{129,1},{2,130},{130,2},{3,131},{131,3},{4... | collective-permute-start | bytes 638984 | tf_op jit(solution)/shard_map/ppermute | solution.py:102

commit v2 on v1

v2 whole, which is shorter than its diff:
```python
import jax
import jax.numpy as jnp
import numpy as np
from jax import lax
from jax.sharding import Mesh, PartitionSpec as P


momentum_decay = 0.9
step_size = 0.05

SWAP = [(0, 1), (1, 0)]


def after(value, *others):
    return lax.optimization_barrier((value, *others))[0]


def placed(index, mine, other, axis, shape):
    return jnp.where(lax.broadcasted_iota(jnp.int32, shape, axis) == index, mine, other)


def halves(mine, other, index):
    def entry(i):
        at = (lax.dynamic_index_in_dim(a, i, 0, keepdims=False) for a in (mine, other))
        return sum(a.astype(jnp.float32) for a in at)

    return lax.optimization_barrier((entry(index), entry(1 - index).astype(jnp.bfloat16)))


def step(activations, weight, out_grad, momentum):
    slab_rows = momentum.shape[1]
    tokens, hid = activations.shape
    own_tokens, cols = out_grad.shape
    n_x = tokens // own_tokens // 2
    half = cols // 2
    part = half // 2
    core, z_hi, z_lo = (lax.axis_index(a) for a in ("core", "z_hi", "z_lo"))

    shape = (n_x, 2, 2, own_tokens, part)
    sent = placed(0, out_grad[:, :part], out_grad[:, part : 2 * part], 1, shape)
    gathered0 = lax.all_to_all(
        sent.reshape(4 * n_x, own_tokens, part),
        ("x", "core", "z_hi"),
        split_axis=0,
        concat_axis=0,
        tiled=True,
    )

    far = lax.ppermute(out_grad[:, 2 * part :], "z_hi", SWAP)
    by_core = [
        placed(z_hi, out_grad[:, 2 * part :][:, c], far[:, c], 2, shape)
        for c in (slice(0, part), slice(part, 2 * part))
    ]
    sent = placed(0, *by_core, 1, shape)
    gathered1 = lax.all_to_all(
        after(sent, gathered0).reshape(2 * n_x, 2, own_tokens, part),
        ("x", "core"),
        split_axis=0,
        concat_axis=0,
        tiled=True,
    )

    partner_act = lax.ppermute(activations, "core", SWAP)
    both_act = placed(
        core,
        activations.reshape(n_x, 1, 2 * own_tokens, hid),
        partner_act.reshape(n_x, 1, 2 * own_tokens, hid),
        1,
        (n_x, 2, 2 * own_tokens, hid),
    ).reshape(2 * tokens, hid)
    both_act = lax.optimization_barrier(both_act)

    partial_out = jnp.dot(activations, weight, preferred_element_type=jnp.float32)
    partial_out = partial_out.astype(jnp.bfloat16).reshape(n_x, 2, own_tokens, cols)
    keep_out = lax.dynamic_index_in_dim(partial_out, z_hi, 1, keepdims=False)
    give = lax.dynamic_index_in_dim(partial_out, 1 - z_hi, 1, keepdims=False)
    got_out = lax.ppermute(after(give, far), "z_hi", SWAP)

    bits = (z_lo // 2, z_lo % 2)
    own_part, got_part = [], []
    for p, gathered in enumerate((gathered0, gathered1)):
        if p > 0:
            gathered = after(gathered, cut)
        local_grad = lax.dot_general(
            both_act,
            gathered.reshape(2 * tokens, part),
            (((0,), (0,)), ((), ())),
            preferred_element_type=jnp.float32,
        )
        slabs = local_grad.astype(jnp.bfloat16).reshape(2, 2, 2, slab_rows, part)
        keep = lax.dynamic_index_in_dim(slabs, bits[1], 1, keepdims=False)
        give = lax.dynamic_index_in_dim(slabs, 1 - bits[1], 1, keepdims=False)
        keep, give = lax.optimization_barrier((keep, give))
        cut = give
        got = lax.ppermute(give, "z_lo", [(i, i ^ 1) for i in range(4)])
        if p > 0:
            keep = after(keep, mid)
        keep, give = halves(keep, got, bits[0])
        mid = give
        got = lax.ppermute(give, "z_lo", [(i, i ^ 2) for i in range(4)])
        if p > 0:
            keep = after(keep, end)
        keep, give = halves(keep, got, core)
        end = give
        own_part.append(keep)
        got_part.append(lax.ppermute(give, "core", SWAP).astype(jnp.float32))

    paired = (keep_out.astype(jnp.float32) + got_out.astype(jnp.float32)).astype(jnp.bfloat16)
    pieces = lax.all_to_all(after(paired, gathered1), "x", split_axis=0, concat_axis=0, tiled=True)
    summed = jnp.sum(pieces.astype(jnp.float32), axis=0).astype(jnp.bfloat16)

    grad_share = jnp.concatenate(
        [
            piece
            for own, got in zip(own_part, got_part)
            for piece in (jnp.where(core == 0, own, got), jnp.where(core == 0, got, own))
        ],
        axis=1,
    )
    new_momentum = momentum_decay * momentum + grad_share[None]
    own_rows = lax.dynamic_slice_in_dim(weight, (z_lo * 2 + core) * slab_rows, slab_rows, 0)
    new_weight = (own_rows.astype(jnp.float32)[None] - step_size * new_momentum).astype(
        jnp.bfloat16
    )
    return (summed, new_momentum, new_weight)


def solution(mesh):
    n_dp, n_hidden, n_mp = (mesh.shape[a] for a in ("dp", "hidden", "mp"))
    grid = np.asarray(mesh.devices).reshape(n_dp // 2, 2, n_hidden // 2, 2, n_mp)
    finer = Mesh(grid, ("z_lo", "core", "x", "z_hi", "mp"))
    dp, hidden = ("z_lo", "core"), ("x", "z_hi")
    return jax.shard_map(
        step,
        mesh=finer,
        in_specs=(P(dp, hidden), P(hidden, "mp"), P(dp + hidden, "mp"), P(dp, hidden, "mp")),
        out_specs=(P(dp + hidden, "mp"), P(dp, hidden, "mp"), P(dp, hidden, "mp")),
        check_vma=False,
    )
```

time: 140 us -> 139 us (level)
  the two profiles are of different devices: /device:TPU:1 before, /device:TPU:192 now
where the time goes in v2:
time: 139 us; the launch traced here: 138 us
  starting transfers between devices  82.7 us (59%)
  waiting for transfers between devices  25.4 us (18%)
  other arithmetic  14.2 us (10%)
  matrix products  9.51 us (7%)
  local copies, waits for them, and re-layouts  5 us (4%)
    ppermute x2, starting transfers between devices, step(): got = lax.ppermute(give, 'z_lo', [(i, i ^ 2) for i in range(4)])  22 us
    all_to_all x1, starting transfers between devices, step(): lax.all_to_all(sent.reshape(4 * n_x, own_tokens, part), ('x', 'core', 'z_...  18.6 us
    all_to_all x1, starting transfers between devices, step(): lax.all_to_all(after(paired, gathered1), 'x', split_axis=0, concat_axis=0...  14.1 us
    ppermute x1, starting transfers between devices, step(): far = lax.ppermute(out_grad[:, 2 * part:], 'z_hi', SWAP)  7.52 us
    all_to_all x1, waiting for transfers between devices, step(): lax.all_to_all(after(paired, gathered1), 'x', split_axis=0, concat_axis=0...  7.04 us
    ppermute x1, waiting for transfers between devices, step(): far = lax.ppermute(out_grad[:, 2 * part:], 'z_hi', SWAP)  6.76 us
    ppermute x2, starting transfers between devices, step(): got = lax.ppermute(give, 'z_lo', [(i, i ^ 1) for i in range(4)])  5.48 us
    all_to_all x1, starting transfers between devices, step(): lax.all_to_all(after(sent, gathered0).reshape(2 * n_x, 2, own_tokens, par...  5.46 us
  transfers between devices with their start and end apart: 12, of which 9 were waited for; matrix products, arithmetic and copies ran while one was open for 19% of the time, Pallas kernels for 0%

profile of v2, /device:TPU:192, one launch (start us, length us, event | category | flops | bytes accessed | tf_op | source)
XLA Modules:
  0.0 137.7 jit_solution(9601435021573604004)
XLA Ops:
  0.6 0.0 copy-start
  0.6 2.1 %collective-permute-start.2 = (bf16[512,1664]{1,0:T(8,128)(2,1)}, bf16[512,1664]{1,0:T(8,128)(2,1)S(1)}, u32[]{:S(2)}, u32[]{:S(2)}) collective-permute-start(bf16[512,1664]{1,0:T(8,128)(2,1)} %param.4), channel_id=1, source_target_pairs={{0,128},{128,0},{1,129},{129,1},{2,130},{130,2},{3,131},{131,3},{4... | collective-permute-start | bytes 5111816 | tf_op jit(solution)/shard_map/ppermute | solution.py:63
  2.7 0.8 fusion.8
  3.5 0.1 iota.38
  3.6 0.1 iota.39
  3.7 0.9 broadcast_select_fusion
  4.6 18.6 %all-to-all-start = ((bf16[32,32,256]{2,1,0:T(8,128)(2,1)}), bf16[32,32,256]{2,1,0:T(8,128)(2,1)}, u32[]{:S(2)}, u32[]{:S(2)}) async-start(bf16[32,32,256]{2,1,0:T(8,128)(2,1)} %broadcast_select_fusion), calls=%async_computation | async-start | bytes 1048576 | tf_op jit(solution)/shard_map/all_to_all | solution.py:41
  23.2 0.8 slice.25
  23.9 7.5 %collective-permute-start = (bf16[32,512]{1,0:T(8,128)(2,1)S(1)}, bf16[32,512]{1,0:T(8,128)(2,1)S(1)}, u32[]{:S(2)}, u32[]{:S(2)}) collective-permute-start(bf16[32,512]{1,0:T(8,128)(2,1)S(1)} %slice.25), channel_id=1, source_target_pairs={{0,8},{8,0},{1,9},{9,1},{2,10},{10,2},{3,11},{11,3},{4,12},{12,4},... | collective-permute-start | bytes 98312 | tf_op jit(solution)/shard_map/ppermute | solution.py:49
  31.5 0.1 iota.42
  31.6 0.1 iota.43
  31.7 6.8 %collective-permute-done = bf16[32,512]{1,0:T(8,128)(2,1)S(1)} collective-permute-done((bf16[32,512]{1,0:T(8,128)(2,1)S(1)}, bf16[32,512]{1,0:T(8,128)(2,1)S(1)}, u32[]{:S(2)}, u32[]{:S(2)}) %collective-permute-start) | collective-permute-done | bytes 32800 | tf_op jit(solution)/shard_map/ppermute | solution.py:49
  38.4 0.9 select_select_fusion
  39.3 4.1 %all-to-all-done = bf16[32,32,256]{2,1,0:T(8,128)(2,1)} async-done(((bf16[32,32,256]{2,1,0:T(8,128)(2,1)}), bf16[32,32,256]{2,1,0:T(8,128)(2,1)}, u32[]{:S(2)}, u32[]{:S(2)}) %all-to-all-start) | async-done | bytes 524320 | tf_op jit(solution)/shard_map/all_to_all | solution.py:41
  43.4 5.5 %all-to-all-start.1 = ((bf16[16,2,32,256]{3,2,1,0:T(8,128)(2,1)}), bf16[16,2,32,256]{3,2,1,0:T(8,128)(2,1)}, u32[]{:S(2)}, u32[]{:S(2)}) async-start(bf16[16,2,32,256]{3,2,1,0:T(8,128)(2,1)} %bitcast.3), calls=%async_computation.1 | async-start | bytes 1048576 | tf_op jit(solution)/shard_map/all_to_all | solution.py:55
  48.9 0.0 copy-done
  48.9 0.0 copy-start.1
  48.9 5.1 %convolution_convert_fusion.2 = bf16[512,1024]{1,0:T(8,128)(2,1)} fusion(bf16[512,1664]{1,0:T(8,128)(2,1)S(1)} %copy-done, bf16[1664,1024]{1,0:T(8,128)(2,1)} %param.5), kind=kOutput, calls=%fused_computation.3 | convolution fusion | flops 1745354752 | bytes 6160384 | tf_op jit(solution)/shard_map/dot_general | solution.py:73
  54.0 0.0 collective-permute-done.2
  54.1 0.0 copy-start.2
  54.1 1.2 copy-done.2
  55.3 0.0 copy-done.1
  55.3 2.1 %bitcast_select_fusion = bf16[1024,1664]{1,0:T(8,128)(2,1)S(1)} fusion(pred[1024]{0:T(1024)(128)(4,1)S(1)} %iota.43, bf16[8,64,1664]{2,1,0:T(8,128)(2,1)} %bitcast.56, bf16[8,64,1664]{2,1,0:T(8,128)(2,1)S(1)} %bitcast.55), kind=kLoop, calls=%fused_computation | loop fusion | flops 1703936 | bytes 6816768 | tf_op jit(solution)/shard_map/jit(_where)/select_n | solution.py:19
  57.4 2.1 %convolution_convert_fusion.1 = bf16[1664,256]{1,0:T(8,128)(2,1)S(1)} fusion(bf16[1024,1664]{1,0:T(8,128)(2,1)S(1)} %bitcast_select_fusion, bf16[1024,256]{1,0:T(8,128)(2,1)} %bitcast.8), kind=kOutput, calls=%fused_computation.2 | convolution fusion | flops 872841216 | bytes 4784128 | tf_op jit(solution)/shard_map/dot_general | solution.py:84
  59.6 1.0 dynamic-slice_bitcast_fusion.3
  60.5 2.7 %collective-permute-start.3 = (bf16[2,2,208,256]{3,2,1,0:T(8,128)(2,1)}, bf16[2,2,208,256]{3,2,1,0:T(8,128)(2,1)}, u32[]{:S(2)}, u32[]{:S(2)}) collective-permute-start(bf16[2,2,208,256]{3,2,1,0:T(8,128)(2,1)} %get-tuple-element.25), channel_id=1, source_target_pairs={{0,256},{256,0},{512,768},{768,512},{1,257},{257,1},{513,769},{769... | collective-permute-start | bytes 1277960 | tf_op jit(solution)/shard_map/ppermute | solution.py:95
  63.2 1.7 %all-to-all-done.1 = bf16[16,2,32,256]{3,2,1,0:T(8,128)(2,1)} async-done(((bf16[16,2,32,256]{3,2,1,0:T(8,128)(2,1)}), bf16[16,2,32,256]{3,2,1,0:T(8,128)(2,1)}, u32[]{:S(2)}, u32[]{:S(2)}) %all-to-all-start.1) | async-done | bytes 524320 | tf_op jit(solution)/shard_map/all_to_all | solution.py:55
  64.9 0.0 copy-start.3
  64.9 2.2 %convolution_convert_fusion = bf16[1664,256]{1,0:T(8,128)(2,1)S(1)} fusion(bf16[1024,1664]{1,0:T(8,128)(2,1)S(1)} %bitcast_select_fusion, bf16[1024,256]{1,0:T(8,128)(2,1)} %bitcast.16), kind=kOutput, calls=%fused_computation.1 | convolution fusion | flops 872841216 | bytes 4784128 | tf_op jit(solution)/shard_map/dot_general | solution.py:84
  67.1 0.0 copy-start.4
  67.1 0.1 dynamic-slice_bitcast_fusion.1
  67.2 2.8 %collective-permute-start.6 = (bf16[2,2,208,256]{3,2,1,0:T(8,128)(2,1)S(1)}, bf16[2,2,208,256]{3,2,1,0:T(8,128)(2,1)}, u32[]{:S(2)}, u32[]{:S(2)}) collective-permute-start(bf16[2,2,208,256]{3,2,1,0:T(8,128)(2,1)S(1)} %get-tuple-element.33), channel_id=1, source_target_pairs={{0,256},{256,0},{512,768},{768,512},{1,257},{257,1},{513,769},{769... | collective-permute-start | bytes 1277960 | tf_op jit(solution)/shard_map/ppermute | solution.py:95
  70.0 0.0 copy-done.3
  70.0 0.8 dynamic-slice_bitcast_fusion
  70.9 3.3 %collective-permute-start.1 = (bf16[8,32,1024]{2,1,0:T(8,128)(2,1)}, bf16[8,32,1024]{2,1,0:T(8,128)(2,1)}, u32[]{:S(2)}, u32[]{:S(2)}) collective-permute-start(bf16[8,32,1024]{2,1,0:T(8,128)(2,1)} %dynamic-slice_bitcast_fusion), channel_id=1, source_target_pairs={{0,8},{8,0},{1,9},{9,1},{2,10},{10,2},{3,11},{11,3},{4,12},{12,4},... | collective-permute-start | bytes 1572872 | tf_op jit(solution)/shard_map/ppermute | solution.py:77
  74.2 1.2 collective-permute-done.3
  75.4 1.3 fusion.3
  76.8 0.0 copy-start.5
  76.8 5.3 %collective-permute-start.4 = (bf16[2,208,256]{2,1,0:T(8,128)(2,1)S(1)}, bf16[2,208,256]{2,1,0:T(8,128)(2,1)}, u32[]{:S(2)}, u32[]{:S(2)}) collective-permute-start(bf16[2,208,256]{2,1,0:T(8,128)(2,1)S(1)} %get-tuple-element.27), channel_id=1, source_target_pairs={{0,512},{256,768},{512,0},{768,256},{1,513},{257,769},{513,1},{769... | collective-permute-start | bytes 638984 | tf_op jit(solution)/shard_map/ppermute | solution.py:100
  82.1 2.5 %collective-permute-done.6 = bf16[2,2,208,256]{3,2,1,0:T(8,128)(2,1)} collective-permute-done((bf16[2,2,208,256]{3,2,1,0:T(8,128)(2,1)S(1)}, bf16[2,2,208,256]{3,2,1,0:T(8,128)(2,1)}, u32[]{:S(2)}, u32[]{:S(2)}) %collective-permute-start.6) | collective-permute-done | bytes 426016 | tf_op jit(solution)/shard_map/ppermute | solution.py:95
  84.5 1.8 %fusion.4 = (bf16[2,208,256]{2,1,0:T(8,128)(2,1)}, f32[2,208,256]{2,1,0:T(8,128)S(1)}) fusion(bf16[2,2,208,256]{3,2,1,0:T(8,128)(2,1)} %collective-permute-done.6, s32[]{:T(128)S(6)} %select_n.110, bf16[2,2,208,256]{3,2,1,0:T(8,128)(2,1)S(1)} %get-tuple-element.32, s32[]{:T(128)S(6)} %select_n.109), kind=kLoop, calls=%fused_computation.26 | loop fusion | flops 745472 | bytes 1490952 | tf_op jit(solution)/shard_map/convert_element_type | solution.py:27
  86.4 16.7 %collective-permute-start.7 = (bf16[2,208,256]{2,1,0:T(8,128)(2,1)}, bf16[2,208,256]{2,1,0:T(8,128)(2,1)}, u32[]{:S(2)}, u32[]{:S(2)}) collective-permute-start(bf16[2,208,256]{2,1,0:T(8,128)(2,1)} %get-tuple-element.36), channel_id=1, source_target_pairs={{0,512},{256,768},{512,0},{768,256},{1,513},{257,769},{513,1},{769... | collective-permute-start | bytes 638984 | tf_op jit(solution)/shard_map/ppermute | solution.py:100
  103.1 1.1 collective-permute-done.1
  104.2 0.0 copy-done.4
  104.2 2.1 %fusion = bf16[8,32,1024]{2,1,0:T(8,128)(2,1)} fusion(bf16[8,32,1024]{2,1,0:T(8,128)(2,1)} %collective-permute-done.1, bf16[8,2,32,1024]{3,2,1,0:T(8,128)(2,1)S(1)} %bitcast.58, s32[]{:T(128)S(6)} %select_n.97), kind=kLoop, calls=%fused_computation.5 | loop fusion | flops 1048576 | bytes 1572868 | tf_op jit(solution)/shard_map/convert_element_type | solution.py:108
  106.2 14.1 %all-to-all-start.2 = ((bf16[8,32,1024]{2,1,0:T(8,128)(2,1)}), bf16[8,32,1024]{2,1,0:T(8,128)(2,1)S(1)}, u32[]{:S(2)}, u32[]{:S(2)}) async-start(bf16[8,32,1024]{2,1,0:T(8,128)(2,1)} %fusion), calls=%async_computation.2 | async-start | bytes 1048576 | tf_op jit(solution)/shard_map/all_to_all | solution.py:109
  120.4 0.0 collective-permute-done.4
  120.4 1.0 fusion.5
  121.4 1.9 %collective-permute-start.5 = (bf16[208,256]{1,0:T(8,128)(2,1)S(1)}, bf16[208,256]{1,0:T(8,128)(2,1)S(1)}, u32[]{:S(2)}, u32[]{:S(2)}) collective-permute-start(bf16[208,256]{1,0:T(8,128)(2,1)S(1)} %get-tuple-element.29), channel_id=1, source_target_pairs={{0,128},{128,0},{1,129},{129,1},{2,130},{130,2},{3,131},{131,3},{4... | collective-permute-start | bytes 319496 | tf_op jit(solution)/shard_map/ppermute | solution.py:106
  123.3 0.2 collective-permute-done.7
  123.5 1.0 fusion.6
  124.5 2.3 %collective-permute-start.8 = (bf16[208,256]{1,0:T(8,128)(2,1)S(1)}, bf16[208,256]{1,0:T(8,128)(2,1)S(1)}, u32[]{:S(2)}, u32[]{:S(2)}) collective-permute-start(bf16[208,256]{1,0:T(8,128)(2,1)S(1)} %get-tuple-element.38), channel_id=1, source_target_pairs={{0,128},{128,0},{1,129},{129,1},{2,130},{130,2},{3,131},{131,3},{4... | collective-permute-start | bytes 319496 | tf_op jit(solution)/shard_map/ppermute | solution.py:106
  126.7 0.0 collective-permute-done.5
  126.8 0.9 collective-permute-done.8
  127.7 0.0 copy-done.5
  127.7 2.2 %fusion.2 = (bf16[1,208,1024]{2,1,0:T(8,128)(2,1)}, f32[1,208,1024]{2,1,0:T(8,128)}) fusion(bf16[1664,1024]{1,0:T(8,128)(2,1)} %param.5, s32[]{:T(128)S(6)} %select_n.117, f32[208,256]{1,0:T(8,128)S(1)} %get-tuple-element.56, f32[208,256]{1,0:T(8,128)S(1)} %get-tuple-element.55, f32[208,256]{1,0:T(8,128)S(1)} %get-tuple-element.54, ...), kind=kLoop, calls=%fused_computation.9 | loop fusion | flops 1916928 | bytes 3407876 | tf_op jit(solution)/shard_map/convert_element_type | solution.py:122
  130.0 7.0 %all-to-all-done.2 = bf16[8,32,1024]{2,1,0:T(8,128)(2,1)S(1)} async-done(((bf16[8,32,1024]{2,1,0:T(8,128)(2,1)}), bf16[8,32,1024]{2,1,0:T(8,128)(2,1)S(1)}, u32[]{:S(2)}, u32[]{:S(2)}) %all-to-all-start.2) | async-done | bytes 524320 | tf_op jit(solution)/shard_map/all_to_all | solution.py:109
  137.0 0.7 reduce_sum.12
  (6 shorter events, 0.1 us)
Async XLA Ops:
  0.6 48.3 %copy-start = (bf16[512,1664]{1,0:T(8,128)(2,1)S(1)}, bf16[512,1664]{1,0:T(8,128)(2,1)}, u32[]{:S(2)}) copy-start(bf16[512,1664]{1,0:T(8,128)(2,1)} %param.4) | copy-start | bytes 5111812
  0.6 53.4 %collective-permute-start.2 = (bf16[512,1664]{1,0:T(8,128)(2,1)}, bf16[512,1664]{1,0:T(8,128)(2,1)S(1)}, u32[]{:S(2)}, u32[]{:S(2)}) collective-permute-start(bf16[512,1664]{1,0:T(8,128)(2,1)} %param.4), channel_id=1, source_target_pairs={{0,128},{128,0},{1,129},{129,1},{2,130},{130,2},{3,131},{131,3},{4... | collective-permute-start | bytes 5111816 | tf_op jit(solution)/shard_map/ppermute | solution.py:63
  4.6 38.8 %all-to-all-start = ((bf16[32,32,256]{2,1,0:T(8,128)(2,1)}), bf16[32,32,256]{2,1,0:T(8,128)(2,1)}, u32[]{:S(2)}, u32[]{:S(2)}) async-start(bf16[32,32,256]{2,1,0:T(8,128)(2,1)} %broadcast_select_fusion), calls=%async_computation | async-start | bytes 1048576 | tf_op jit(solution)/shard_map/all_to_all | solution.py:41
  23.9 14.5 %collective-permute-start = (bf16[32,512]{1,0:T(8,128)(2,1)S(1)}, bf16[32,512]{1,0:T(8,128)(2,1)S(1)}, u32[]{:S(2)}, u32[]{:S(2)}) collective-permute-start(bf16[32,512]{1,0:T(8,128)(2,1)S(1)} %slice.25), channel_id=1, source_target_pairs={{0,8},{8,0},{1,9},{9,1},{2,10},{10,2},{3,11},{11,3},{4,12},{12,4},... | collective-permute-start | bytes 98312 | tf_op jit(solution)/shard_map/ppermute | solution.py:49
  43.4 21.5 %all-to-all-start.1 = ((bf16[16,2,32,256]{3,2,1,0:T(8,128)(2,1)}), bf16[16,2,32,256]{3,2,1,0:T(8,128)(2,1)}, u32[]{:S(2)}, u32[]{:S(2)}) async-start(bf16[16,2,32,256]{3,2,1,0:T(8,128)(2,1)} %bitcast.3), calls=%async_computation.1 | async-start | bytes 1048576 | tf_op jit(solution)/shard_map/all_to_all | solution.py:55
  48.9 6.4 %copy-start.1 = (bf16[512,1664]{1,0:T(8,128)(2,1)S(1)}, bf16[512,1664]{1,0:T(8,128)(2,1)}, u32[]{:S(2)}) copy-start(bf16[512,1664]{1,0:T(8,128)(2,1)} %param.4) | copy-start | bytes 5111812
  54.1 1.2 copy-start.2
  60.5 14.9 %collective-permute-start.3 = (bf16[2,2,208,256]{3,2,1,0:T(8,128)(2,1)}, bf16[2,2,208,256]{3,2,1,0:T(8,128)(2,1)}, u32[]{:S(2)}, u32[]{:S(2)}) collective-permute-start(bf16[2,2,208,256]{3,2,1,0:T(8,128)(2,1)} %get-tuple-element.25), channel_id=1, source_target_pairs={{0,256},{256,0},{512,768},{768,512},{1,257},{257,1},{513,769},{769... | collective-permute-start | bytes 1277960 | tf_op jit(solution)/shard_map/ppermute | solution.py:95
  64.9 5.1 %copy-start.3 = (bf16[512,1024]{1,0:T(8,128)(2,1)S(1)}, bf16[512,1024]{1,0:T(8,128)(2,1)}, u32[]{:S(2)}) copy-start(bf16[512,1024]{1,0:T(8,128)(2,1)} %convolution_convert_fusion.2) | copy-start | bytes 3145732
  67.1 37.1 %copy-start.4 = (bf16[512,1024]{1,0:T(8,128)(2,1)S(1)}, bf16[512,1024]{1,0:T(8,128)(2,1)}, u32[]{:S(2)}) copy-start(bf16[512,1024]{1,0:T(8,128)(2,1)} %convolution_convert_fusion.2) | copy-start | bytes 3145732
  67.2 17.3 %collective-permute-start.6 = (bf16[2,2,208,256]{3,2,1,0:T(8,128)(2,1)S(1)}, bf16[2,2,208,256]{3,2,1,0:T(8,128)(2,1)}, u32[]{:S(2)}, u32[]{:S(2)}) collective-permute-start(bf16[2,2,208,256]{3,2,1,0:T(8,128)(2,1)S(1)} %get-tuple-element.33), channel_id=1, source_target_pairs={{0,256},{256,0},{512,768},{768,512},{1,257},{257,1},{513,769},{769... | collective-permute-start | bytes 1277960 | tf_op jit(solution)/shard_map/ppermute | solution.py:95
  70.9 33.3 %collective-permute-start.1 = (bf16[8,32,1024]{2,1,0:T(8,128)(2,1)}, bf16[8,32,1024]{2,1,0:T(8,128)(2,1)}, u32[]{:S(2)}, u32[]{:S(2)}) collective-permute-start(bf16[8,32,1024]{2,1,0:T(8,128)(2,1)} %dynamic-slice_bitcast_fusion), channel_id=1, source_target_pairs={{0,8},{8,0},{1,9},{9,1},{2,10},{10,2},{3,11},{11,3},{4,12},{12,4},... | collective-permute-start | bytes 1572872 | tf_op jit(solution)/shard_map/ppermute | solution.py:77
  76.8 50.9 %copy-start.5 = (f32[1,208,1024]{2,1,0:T(8,128)S(1)}, f32[1,208,1024]{2,1,0:T(8,128)}, u32[]{:S(2)}) copy-start(f32[1,208,1024]{2,1,0:T(8,128)} %param.7) | copy-start | bytes 2555908
  76.8 43.6 %collective-permute-start.4 = (bf16[2,208,256]{2,1,0:T(8,128)(2,1)S(1)}, bf16[2,208,256]{2,1,0:T(8,128)(2,1)}, u32[]{:S(2)}, u32[]{:S(2)}) collective-permute-start(bf16[2,208,256]{2,1,0:T(8,128)(2,1)S(1)} %get-tuple-element.27), channel_id=1, source_target_pairs={{0,512},{256,768},{512,0},{768,256},{1,513},{257,769},{513,1},{769... | collective-permute-start | bytes 638984 | tf_op jit(solution)/shard_map/ppermute | solution.py:100
  86.4 37.1 %collective-permute-start.7 = (bf16[2,208,256]{2,1,0:T(8,128)(2,1)}, bf16[2,208,256]{2,1,0:T(8,128)(2,1)}, u32[]{:S(2)}, u32[]{:S(2)}) collective-permute-start(bf16[2,208,256]{2,1,0:T(8,128)(2,1)} %get-tuple-element.36), channel_id=1, source_target_pairs={{0,512},{256,768},{512,0},{768,256},{1,513},{257,769},{513,1},{769... | collective-permute-start | bytes 638984 | tf_op jit(solution)/shard_map/ppermute | solution.py:100
  106.2 30.8 %all-to-all-start.2 = ((bf16[8,32,1024]{2,1,0:T(8,128)(2,1)}), bf16[8,32,1024]{2,1,0:T(8,128)(2,1)S(1)}, u32[]{:S(2)}, u32[]{:S(2)}) async-start(bf16[8,32,1024]{2,1,0:T(8,128)(2,1)} %fusion), calls=%async_computation.2 | async-start | bytes 1048576 | tf_op jit(solution)/shard_map/all_to_all | solution.py:109
  121.4 5.4 %collective-permute-start.5 = (bf16[208,256]{1,0:T(8,128)(2,1)S(1)}, bf16[208,256]{1,0:T(8,128)(2,1)S(1)}, u32[]{:S(2)}, u32[]{:S(2)}) collective-permute-start(bf16[208,256]{1,0:T(8,128)(2,1)S(1)} %get-tuple-element.29), channel_id=1, source_target_pairs={{0,128},{128,0},{1,129},{129,1},{2,130},{130,2},{3,131},{131,3},{4... | collective-permute-start | bytes 319496 | tf_op jit(solution)/shard_map/ppermute | solution.py:106
  124.5 3.2 %collective-permute-start.8 = (bf16[208,256]{1,0:T(8,128)(2,1)S(1)}, bf16[208,256]{1,0:T(8,128)(2,1)S(1)}, u32[]{:S(2)}, u32[]{:S(2)}) collective-permute-start(bf16[208,256]{1,0:T(8,128)(2,1)S(1)} %get-tuple-element.38), channel_id=1, source_target_pairs={{0,128},{128,0},{1,129},{129,1},{2,130},{130,2},{3,131},{131,3},{4... | collective-permute-start | bytes 319496 | tf_op jit(solution)/shard_map/ppermute | solution.py:106
